TPU v7x, 32 devices: a whole 2x2x4 slice. The times are simulated.
32 devices in a mesh: rows: 2 (over core), tp: 4 (over y, x), attn: 4 (over z).
Axes of the slice: x: 2, y: 2, z: 4, core: 2. Of those that a mesh axis runs over, the one named last changes fastest.
Arguments:
- tokens: bfloat16 [4096, 4096], P(('rows', 'attn')), may hold values from -60 to 60, as said below
- norm_gain: bfloat16 [4096], replicated, may hold values from 0.099609375 to 1.8984375
- w_query: bfloat16 [4096, 2048], P('rows', 'tp'), may hold values from -1 to 1, as said below
- key_projection_weight: bfloat16 [4096, 512], P('rows', 'tp'), may hold values from -8 to 8, as said below
- value_projection_weight: bfloat16 [4096, 512], P('rows', 'tp'), may hold values from -0.09375 to 0.09375
- documents: int32 [2, 2048], P('rows'), may hold values from 0 to 5, never falling along the last dimension, each value on 1 to 1024 neighbouring positions
Outputs:
- attn_out: bfloat16 [4096, 2048], P(('rows', 'attn'), 'tp')
Inputs may be any that keep to these rules, and one draw needn't show every extreme that they name: `tokens`: activations of order one. `w_query`: entries of order 4096 ** -0.5. `key_projection_weight`: entries of order one or smaller. `documents`: along each window the document numbers never fall; every document spans 1 to 1024 tokens and some document of each window spans exactly 1024.
All inputs are finite; a program needn't handle non-finite values.
Results may differ from a plain program's by a relative error of at most 0.012.
The roundings to bfloat16 on the way count: a program that leaves them out, or rounds other values in their place, can miss the bound.
Values may be sent and summed in bfloat16 or wider, within the bound.
A program may use at most 64 MiB of HBM per device.

v0:
```python
import functools
import math

import jax
import jax.numpy as jnp
import numpy as np
from jax import lax
from jax.experimental import pallas as pl
from jax.experimental.pallas import tpu as pltpu
from jax.sharding import PartitionSpec as P

HEAD = 128
MOST = 1024
TQ = 128
BF16 = jnp.bfloat16
F32 = jnp.float32
MESH = pl.DeviceIdType.MESH


def rotary_table(window):
    half = HEAD // 2
    frequency = np.exp(
        np.arange(half, dtype=np.float32) * np.float32(-2.0 * math.log(500000.0) / HEAD)
    ).astype(np.float32)
    angles = np.arange(window, dtype=np.float32)[:, None] * frequency[None, :]
    return np.concatenate([np.cos(angles), np.sin(angles)], axis=1).astype(np.float32)


def kernel(
    n_rows, n_attn, back, chunk,
    tok, gain, wq, wk, wv, docs, table, out,
    gains, xt, xn, wkv_buf, wq_buf, kv, q, tab, kdoc, qdoc,
    tok_sem, own_sem, w_send, w_recv, kv_send, kv_recv,
):
    rows = tok.shape[0]
    depth = wk.shape[0]
    kvw = wk.shape[1]
    qw = wq.shape[1]
    kv_heads = kvw // HEAD
    group = qw // kvw
    chunks = rows // chunk
    tiles = rows // TQ
    mine = back * rows
    span = min(mine + rows, -(-(MOST - 1 + TQ) // TQ) * TQ)
    me = lax.axis_index("rows")
    at = lax.axis_index("attn")

    tok_copies = [
        pltpu.make_async_copy(
            tok.at[pl.ds(c * chunk, chunk)], xt.at[pl.ds(c * chunk, chunk)], tok_sem.at[c]
        )
        for c in range(chunks)
    ]
    own_copies = [
        pltpu.make_async_copy(wk, wkv_buf.at[0, :, pl.ds(0, kvw)], own_sem.at[0]),
        pltpu.make_async_copy(wv, wkv_buf.at[0, :, pl.ds(kvw, kvw)], own_sem.at[1]),
        pltpu.make_async_copy(wq, wq_buf.at[0], own_sem.at[2]),
        pltpu.make_async_copy(
            table.at[pl.ds(pl.multiple_of(at * rows, rows), rows)], tab, own_sem.at[3]
        ),
    ]
    tok_copies[-1].start()
    own_copies[0].start()
    own_copies[1].start()
    own_copies[3].start()
    for copy in tok_copies[-2::-1]:
        copy.start()

    barrier = pltpu.get_barrier_semaphore()
    for d in range(1, n_rows):
        pl.semaphore_signal(
            barrier, inc=1, device_id={"rows": lax.rem(me + d, n_rows)}, device_id_type=MESH
        )
    has_prev = at > 0
    has_next = at < n_attn - 1
    if back:

        @pl.when(has_prev)
        def _():
            pl.semaphore_signal(
                barrier, inc=1, device_id={"attn": at - 1}, device_id_type=MESH
            )

        @pl.when(has_next)
        def _():
            pl.semaphore_signal(
                barrier, inc=1, device_id={"attn": at + 1}, device_id_type=MESH
            )

        pl.semaphore_wait(
            barrier, n_rows - 1 + has_prev.astype(jnp.int32) + has_next.astype(jnp.int32)
        )
    elif n_rows > 1:
        pl.semaphore_wait(barrier, n_rows - 1)

    def weight_copy(d, which):
        src, dst = (
            (wk, wkv_buf.at[d, :, pl.ds(0, kvw)]),
            (wv, wkv_buf.at[d, :, pl.ds(kvw, kvw)]),
            (wq, wq_buf.at[d]),
        )[which]
        return pltpu.make_async_remote_copy(
            src_ref=src, dst_ref=dst,
            send_sem=w_send.at[d, which], recv_sem=w_recv.at[d, which],
            device_id={"rows": lax.rem(me + d, n_rows)}, device_id_type=MESH,
        )

    for which in range(3):
        for d in range(1, n_rows):
            weight_copy(d, which).start()
    own_copies[2].start()

    for s in range(back + 1):
        block = at - back + s
        keep = pl.multiple_of(jnp.maximum(block, 0) * rows, rows)
        kdoc[:, pl.ds(s * rows, rows)] = jnp.where(block >= 0, docs[:, pl.ds(keep, rows)], -1)
    for t in range(tiles):
        row = kdoc[:, pl.ds(mine + t * TQ, TQ)]
        qdoc[pl.ds(t * TQ, TQ), :] = jnp.broadcast_to(row, (TQ, TQ)).T
    for s in range(back):

        @pl.when(at - back + s < 0)
        def _():
            kv[pl.ds(s * rows, rows), :] = jnp.zeros((rows, 2 * kvw), BF16)

    lane = lax.broadcasted_iota(jnp.int32, (1, HEAD), 1)

    def tables(start, size):
        t = tab[pl.ds(start, size), :]
        swapped = pltpu.roll(t, HEAD // 2, 1)
        low = lane < HEAD // 2
        return jnp.where(low, t, swapped), jnp.where(low, -swapped, t)

    def rotate(u, cosine, sine):
        return (u * cosine + pltpu.roll(u, HEAD // 2, 1) * sine).astype(BF16)

    def project(start, size, weights):
        total = None
        for d in range(n_rows):
            owner = lax.rem(me - d + n_rows, n_rows)
            part = jnp.dot(
                xn[pl.ds(start, size), pl.ds(pl.multiple_of(owner * depth, depth), depth)],
                weights[d],
                preferred_element_type=F32,
            )
            total = part if total is None else total + part
        return total

    def hop(s, c):
        return pltpu.make_async_remote_copy(
            src_ref=kv.at[pl.ds((back - s) * rows + c * chunk, chunk)],
            dst_ref=kv.at[pl.ds((back - s - 1) * rows + c * chunk, chunk)],
            send_sem=kv_send.at[s, c], recv_sem=kv_recv.at[s, c],
            device_id={"attn": jnp.minimum(at + 1, n_attn - 1)}, device_id_type=MESH,
        )

    def arrived(s, c):
        @pl.when(at > s)
        def _():
            hop(s, c).wait_recv()

        if s + 1 < back:

            @pl.when((at > s) & has_next)
            def _():
                hop(s + 1, c).start()

    relayed = [(s, c) for s in range(back - 1) for c in reversed(range(chunks))]
    strip, piece = 16, 256
    width = tok.shape[1]
    gains[...] = jnp.broadcast_to(gain[...].astype(F32).reshape(1, -1), gains.shape)
    for c in reversed(range(chunks)):
        if c == 0 and relayed:
            arrived(*relayed.pop(0))
        tok_copies[c].wait()

        @pl.loop(0, chunk // strip, unroll=4)
        def _(i):
            here = pl.ds(pl.multiple_of(c * chunk + i * strip, strip), strip)
            squares = jnp.zeros((strip, piece), F32)
            for k in range(width // piece):
                x = xt[here, pl.ds(k * piece, piece)].astype(F32)
                squares = squares + x * x
            mean_sq = jnp.sum(squares, axis=-1, keepdims=True) * (1.0 / width)
            scale = jnp.broadcast_to(lax.rsqrt(mean_sq + 1e-05), (strip, piece))
            for k in range(width // piece):
                cols = pl.ds(k * piece, piece)
                x = xt[here, cols].astype(F32) * scale
                xn[here, cols] = (
                    x.reshape(strip // 8, 8, piece) * gains[:, cols][None]
                ).reshape(strip, piece).astype(BF16)

        if c == chunks - 1:
            own_copies[0].wait()
            own_copies[1].wait()
            own_copies[3].wait()
            for d in range(1, n_rows):
                weight_copy(d, 0).wait()
                weight_copy(d, 1).wait()
        total = project(c * chunk, chunk, wkv_buf)
        cosine, sine = tables(c * chunk, chunk)
        here = pl.ds(mine + c * chunk, chunk)
        for h in range(kv_heads):
            kv[here, pl.ds(h * HEAD, HEAD)] = rotate(
                total[:, h * HEAD : (h + 1) * HEAD], cosine, sine
            )
        kv[here, pl.ds(kvw, kvw)] = total[:, kvw:].astype(BF16)
        if back:

            @pl.when(has_next)
            def _():
                hop(0, c).start()

    last = [(back - 1, c) for c in reversed(range(chunks))] if back else []

    own_copies[2].wait()
    for d in range(1, n_rows):
        weight_copy(d, 2).wait()
    part = min(rows, 2 * chunk)
    for step in reversed(range(rows // part)):
        for _ in range(min(1, len(relayed))):
            arrived(*relayed.pop(0))
        total = project(step * part, part, wq_buf)
        cosine, sine = tables(step * part, part)
        for h in range(kv_heads):
            for g in range(group):
                col = (h * group + g) * HEAD
                u = rotate(total[:, col : col + HEAD], cosine, sine)
                for t in range(part // TQ):
                    q[step * (part // TQ) + t, h, pl.ds(g * TQ, TQ), :] = u[
                        t * TQ : (t + 1) * TQ
                    ]
    for event in relayed:
        arrived(*event)

    factor = math.log2(math.e) / math.sqrt(HEAD)

    for t in reversed(range(tiles)):
        first = t * TQ
        begin = max(mine + first + TQ - span, 0)
        while last and (last[0][1] + 1) * chunk > begin:
            arrived(*last.pop(0))
        query_at = lax.broadcasted_iota(jnp.int32, (TQ, 1), 0) + (mine + first)
        key_at = lax.broadcasted_iota(jnp.int32, (1, span), 1) + begin
        visible = (qdoc[pl.ds(first, TQ), :][:, :1] == kdoc[:, pl.ds(begin, span)]) & (
            query_at >= key_at
        )
        for h in range(kv_heads):
            keys = kv[pl.ds(begin, span), pl.ds(h * HEAD, HEAD)]
            vals = kv[pl.ds(begin, span), pl.ds(kvw + h * HEAD, HEAD)]
            s = lax.dot_general(
                q[t, h], keys, (((1,), (1,)), ((), ())), preferred_element_type=F32
            )
            s = jnp.where(visible[None], s.reshape(group, TQ, span), -1e30)
            p = jnp.exp2((s - jnp.max(s, axis=-1, keepdims=True)) * factor)
            total = jnp.sum(p, axis=-1, keepdims=True)
            mixed = jnp.dot(
                p.astype(BF16).reshape(group * TQ, span), vals, preferred_element_type=F32
            )
            mixed = (mixed.reshape(group, TQ, HEAD) / total).astype(BF16)
            for g in range(group):
                out[pl.ds(first, TQ), pl.ds((h * group + g) * HEAD, HEAD)] = mixed[g]
    for event in last:
        arrived(*event)

    for s in range(back):
        for c in range(chunks):

            @pl.when((at >= s) & has_next)
            def _():
                hop(s, c).wait_send()


def solution(mesh):
    n_rows = mesh.shape["rows"]
    n_attn = mesh.shape["attn"]

    def on_device(tokens, norm_gain, w_query, w_key, w_value, documents):
        rows, width = tokens.shape
        depth, qw = w_query.shape
        kvw = w_key.shape[1]
        back = min(n_attn - 1, -(-(MOST - 1) // rows))
        chunk = min(rows, TQ)
        chunks = rows // chunk
        table = jnp.asarray(rotary_table(documents.shape[1]))
        anywhere = pl.BlockSpec(memory_space=pl.ANY)
        vmem = pl.BlockSpec(memory_space=pltpu.VMEM)
        keys = (back + 1) * rows
        group = qw // kvw
        return pl.pallas_call(
            functools.partial(kernel, n_rows, n_attn, back, chunk),
            out_shape=jax.ShapeDtypeStruct((rows, qw), BF16),
            in_specs=[anywhere, vmem, anywhere, anywhere, anywhere, vmem, anywhere],
            out_specs=vmem,
            scratch_shapes=[
                pltpu.VMEM((8, width), F32),
                pltpu.VMEM((rows, width), BF16),
                pltpu.VMEM((rows, width), BF16),
                pltpu.VMEM((n_rows, depth, 2 * kvw), BF16),
                pltpu.VMEM((n_rows, depth, qw), BF16),
                pltpu.VMEM((keys, 2 * kvw), BF16),
                pltpu.VMEM((rows // TQ, kvw // HEAD, group * TQ, HEAD), BF16),
                pltpu.VMEM((rows, HEAD), F32),
                pltpu.VMEM((1, keys), jnp.int32),
                pltpu.VMEM((rows, TQ), jnp.int32),
                pltpu.SemaphoreType.DMA((chunks,)),
                pltpu.SemaphoreType.DMA((4,)),
                pltpu.SemaphoreType.DMA((n_rows, 3)),
                pltpu.SemaphoreType.DMA((n_rows, 3)),
                pltpu.SemaphoreType.DMA((max(back, 1), chunks)),
                pltpu.SemaphoreType.DMA((max(back, 1), chunks)),
            ],
            compiler_params=pltpu.CompilerParams(
                collective_id=0, has_side_effects=True, vmem_limit_bytes=60 << 20
            ),
            name="layer",
        )(tokens, norm_gain, w_query, w_key, w_value, documents, table)

    placed = (
        P(("rows", "attn"), None),
        P(),
        P("rows", "tp"),
        P("rows", "tp"),
        P("rows", "tp"),
        P("rows", None),
    )
    return jax.shard_map(
        on_device, mesh=mesh, in_specs=placed, out_specs=P(("rows", "attn"), "tp"), check_vma=False
    )
```

profile of v0, /device:TPU:18, one launch (start us, length us, event | category | flops | bytes accessed | tf_op | source)
XLA Modules:
  0.0 24.1 jit_solution(4374512135138321318)
XLA Ops:
  0.0 22.2 %layer.1 = bf16[512,512]{1,0:T(8,128)(2,1)} custom-call(bf16[512,4096]{1,0:T(8,128)(2,1)} %tok.1, bf16[4096]{0:T(1024)(128)(2,1)} %gain.1, bf16[2048,512]{1,0:T(8,128)(2,1)} %wq.1, bf16[2048,128]{1,0:T(8,128)(2,1)} %wk.1, bf16[2048,128]{1,0:T(8,128)(2,1)} %wv.1, s32[1,2048]{1,0:T(1,128)} %docs.1, f32[2048,128]{1,0:T(8,128)} %constant.2.clone.table), custom_call_target="tpu_custom_call" | custom-call | tf_op jit(solution)/shard_map/layer/pallas_call | solution.py:290
  22.2 1.9 %copy.9 = bf16[512,512]{1,0:T(8,128)(2,1)} copy(bf16[512,512]{1,0:T(8,128)(2,1)} %layer.1) | data formatting | bytes 1048576
where the time goes:
time: 24.3 us; the launch traced here: 24.1 us
  Pallas kernels  22.2 us (91%)
  local copies, waits for them, and re-layouts  1.87 us (8%)
    pallas_call x1, Pallas kernels, on_device(): pl.pallas_call(functools.partial(kernel, n_rows, n_attn, back, chunk), ou...  22.2 us
    unnamed x1, local copies, waits for them, and re-layouts  1.87 us

commit v1 on v0

--- a/solution.py
+++ b/solution.py
@@ -289,7 +289,7 @@
         group = qw // kvw
         return pl.pallas_call(
             functools.partial(kernel, n_rows, n_attn, back, chunk),
-            out_shape=jax.ShapeDtypeStruct((rows, qw), BF16),
+            out_shape=pltpu.VMEM((rows, qw), BF16),
             in_specs=[anywhere, vmem, anywhere, anywhere, anywhere, vmem, anywhere],
             out_specs=vmem,
             scratch_shapes=[
@@ -311,10 +311,10 @@
                 pltpu.SemaphoreType.DMA((max(back, 1), chunks)),
             ],
             compiler_params=pltpu.CompilerParams(
-                collective_id=0, has_side_effects=True, vmem_limit_bytes=60 << 20
+                collective_id=0, has_side_effects=True, vmem_limit_bytes=40 << 20
             ),
             name="layer",
-        )(tokens, norm_gain, w_query, w_key, w_value, documents, table)
+        )(*(pltpu.with_memory_space_constraint(a, pltpu.HBM) for a in (tokens, norm_gain, w_query, w_key, w_value, documents, table)))
 
     placed = (
         P(("rows", "attn"), None),

time: 24.3 us -> 22.5 us (0.926)
  local copies, waits for them, and re-layouts: 1.87 us -> 0.8 us
  Pallas kernels: 22.2 us -> 21.4 us
    unnamed x1, local copies, waits for them, and re-layouts: 1.87 us -> 0.8 us
    pallas_call x1, Pallas kernels: 22.2 us -> 21.4 us  [on_device(): pl.pallas_call(functools.partial(kernel, n_rows, n_attn, back, chunk), ou...]
where the time goes in v1:
time: 22.5 us; the launch traced here: 22.2 us
  Pallas kernels  21.4 us (95%)
  local copies, waits for them, and re-layouts  0.8 us (4%)
    pallas_call x1, Pallas kernels, on_device(): pl.pallas_call(functools.partial(kernel, n_rows, n_attn, back, chunk), ou...  21.4 us
    unnamed x1, local copies, waits for them, and re-layouts  0.8 us

profile of v1, /device:TPU:18, one launch (start us, length us, event | category | flops | bytes accessed | tf_op | source)
XLA Modules:
  0.0 22.2 jit_solution(13639934834330195428)
XLA Ops:
  0.0 21.4 %layer.1 = bf16[512,512]{1,0:T(8,128)(2,1)S(1)} custom-call(bf16[512,4096]{1,0:T(8,128)(2,1)} %tok.1, bf16[4096]{0:T(1024)(128)(2,1)} %gain.1, bf16[2048,512]{1,0:T(8,128)(2,1)} %wq.1, bf16[2048,128]{1,0:T(8,128)(2,1)} %wk.1, bf16[2048,128]{1,0:T(8,128)(2,1)} %wv.1, s32[1,2048]{1,0:T(1,128)} %docs.1, f32[2048,128]{1,0:T(8,128)} %constant.2.clone.table), custom_call_target="tpu_custom_call" | custom-call | tf_op jit(solution)/shard_map/layer/pallas_call | solution.py:290
  21.4 0.8 %copy.9 = bf16[512,512]{1,0:T(8,128)(2,1)} copy(bf16[512,512]{1,0:T(8,128)(2,1)S(1)} %layer.1) | data formatting | bytes 1048576

commit v2 on v1

v2 whole, which is shorter than its diff:
```python
import functools
import math

import jax
import jax.numpy as jnp
import numpy as np
from jax import lax
from jax.experimental import pallas as pl
from jax.experimental.pallas import tpu as pltpu
from jax.sharding import PartitionSpec as P

HEAD = 128
MOST = 1024
TQ = 128
BF16 = jnp.bfloat16
F32 = jnp.float32
MESH = pl.DeviceIdType.MESH


def rotary_table(window):
    half = HEAD // 2
    frequency = np.exp(
        np.arange(half, dtype=np.float32) * np.float32(-2.0 * math.log(500000.0) / HEAD)
    ).astype(np.float32)
    angles = np.arange(window, dtype=np.float32)[:, None] * frequency[None, :]
    return np.concatenate([np.cos(angles), np.sin(angles)], axis=1).astype(np.float32)


def kernel(
    n_rows, n_attn, back, block, part,
    tok, gain, wq, wk, wv, docs, table, out,
    gains, xt, xn, wkv_buf, wq_buf, kbuf, vbuf, q, tops, acc, tab, kdoc, qdoc,
    tok_sem, own_sem, w_send, w_recv, kv_send, kv_recv, ready,
):
    rows, width = tok.shape
    depth, kvw = wk.shape
    qw = wq.shape[1]
    kv_heads = kvw // HEAD
    group = qw // kvw
    parts = qw // part
    tiles = rows // TQ
    mine = back * rows
    span = min(mine + rows, -(-(MOST - 1 + TQ) // TQ) * TQ)
    me = lax.axis_index("rows")
    at = lax.axis_index("attn")
    has_prev = at > 0
    has_next = at < n_attn - 1

    def tok_copy(c):
        here = pl.ds(c * TQ, TQ)
        return pltpu.make_async_copy(tok.at[here], xt.at[here], tok_sem.at[c])

    weights = [
        (wk, lambda d: wkv_buf.at[d, :, pl.ds(0, kvw)]),
        (wv, lambda d: wkv_buf.at[d, :, pl.ds(kvw, kvw)]),
    ] + [
        (wq.at[:, pl.ds(j * part, part)], lambda d, j=j: wq_buf.at[j, d]) for j in range(parts)
    ]

    def own_copy(i):
        src, dst = weights[i]
        return pltpu.make_async_copy(src, dst(0), own_sem.at[i])

    def weight_copy(d, i):
        src, dst = weights[i]
        return pltpu.make_async_remote_copy(
            src_ref=src, dst_ref=dst(d),
            send_sem=w_send.at[d, i], recv_sem=w_recv.at[d, i],
            device_id={"rows": lax.rem(me + d, n_rows)}, device_id_type=MESH,
        )

    tab_copy = pltpu.make_async_copy(
        table.at[pl.ds(pl.multiple_of(at * rows, rows), rows)], tab, own_sem.at[len(weights)]
    )

    tok_copy(tiles - 1).start()
    own_copy(0).start()
    for c in reversed(range(tiles - 1)):
        tok_copy(c).start()
        if c == tiles - 2:
            tab_copy.start()
            own_copy(1).start()

    barrier = pltpu.get_barrier_semaphore()
    paired = n_rows == 2 and n_attn > 1
    if paired:
        first = me == 0

        @pl.when(jnp.logical_not(first))
        def _():
            pl.semaphore_signal(barrier, inc=1, device_id={"rows": 0}, device_id_type=MESH)

        @pl.when(first)
        def _():
            pl.semaphore_wait(barrier, 1)
            pl.semaphore_signal(ready, inc=1, device_id={"rows": 1}, device_id_type=MESH)

        @pl.when(jnp.logical_not(first))
        def _():
            pl.semaphore_wait(ready, 1)
    else:
        for d in range(1, n_rows):
            pl.semaphore_signal(
                barrier, inc=1, device_id={"rows": lax.rem(me + d, n_rows)}, device_id_type=MESH
            )
        if back:

            @pl.when(has_prev)
            def _():
                pl.semaphore_signal(
                    barrier, inc=1, device_id={"attn": at - 1}, device_id_type=MESH
                )

            pl.semaphore_wait(barrier, n_rows - 1 + has_next.astype(jnp.int32))
        elif n_rows > 1:
            pl.semaphore_wait(barrier, n_rows - 1)

    for i in range(len(weights)):
        for d in range(1, n_rows):
            weight_copy(d, i).start()
    if paired:

        @pl.when(has_prev)
        def _():
            pl.semaphore_signal(
                barrier, inc=1, device_id={"rows": 1, "attn": at - 1}, device_id_type=MESH
            )

    for i in range(2, len(weights)):
        own_copy(i).start()

    for s in range(back + 1):
        owner = at - back + s
        keep = pl.multiple_of(jnp.maximum(owner, 0) * rows, rows)
        kdoc[:, pl.ds(s * rows, rows)] = jnp.where(owner >= 0, docs[:, pl.ds(keep, rows)], -1)
    for t in range(tiles):
        row = kdoc[:, pl.ds(mine + t * TQ, TQ)]
        qdoc[pl.ds(t * TQ, TQ), :] = jnp.broadcast_to(row, (TQ, TQ)).T
    for s in range(back):

        @pl.when(at - back + s < 0)
        def _():
            kbuf[pl.ds(s * rows, rows), :] = jnp.zeros((rows, kvw), BF16)
            vbuf[pl.ds(s * rows, rows), :] = jnp.zeros((rows, kvw), BF16)

    gains[...] = jnp.broadcast_to(gain[...].astype(F32).reshape(1, -1), gains.shape)

    pieces = [(which, rows - block, block) for which in range(2)]
    for c in reversed(range((rows - block) // TQ)):
        pieces += [(which, c * TQ, TQ) for which in range(2)]

    def hop(s, p):
        which, start, size = pieces[p]
        ref = (kbuf, vbuf)[which]
        return pltpu.make_async_remote_copy(
            src_ref=ref.at[pl.ds((back - s) * rows + start, size)],
            dst_ref=ref.at[pl.ds((back - s - 1) * rows + start, size)],
            send_sem=kv_send.at[s, p], recv_sem=kv_recv.at[s, p],
            device_id={"attn": jnp.minimum(at + 1, n_attn - 1)}, device_id_type=MESH,
        )

    def send(wanted):
        if back:

            @pl.when(has_next)
            def _():
                for p in wanted:
                    hop(0, p).start()

    def arrived(s, p):
        @pl.when(at > s)
        def _():
            hop(s, p).wait_recv()

        if s + 1 < back:

            @pl.when((at > s) & has_next)
            def _():
                hop(s + 1, p).start()

    relays = [(s, p) for s in range(back - 1) for p in range(len(pieces))]
    last = [(back - 1, p) for p in range(len(pieces))] if back else []

    def relay(count):
        for _ in range(min(count, len(relays))):
            arrived(*relays.pop(0))

    strip, piece = 16, 256

    def norm(c):
        tok_copy(c).wait()

        @pl.loop(0, TQ // strip, unroll=4)
        def _(i):
            here = pl.ds(pl.multiple_of(c * TQ + i * strip, strip), strip)
            squares = jnp.zeros((strip, piece), F32)
            for k in range(width // piece):
                x = xt[here, pl.ds(k * piece, piece)].astype(F32)
                squares = squares + x * x
            mean_sq = jnp.sum(squares, axis=-1, keepdims=True) * (1.0 / width)
            scale = jnp.broadcast_to(lax.rsqrt(mean_sq + 1e-05), (strip, piece))
            for k in range(width // piece):
                cols = pl.ds(k * piece, piece)
                x = xt[here, cols].astype(F32) * scale
                xn[here, cols] = (
                    x.reshape(strip // 8, 8, piece) * gains[:, cols][None]
                ).reshape(strip, piece).astype(BF16)

    lane = lax.broadcasted_iota(jnp.int32, (1, HEAD), 1)

    def tables(start, size):
        t = tab[pl.ds(start, size), :]
        swapped = pltpu.roll(t, HEAD // 2, 1)
        low = lane < HEAD // 2
        return jnp.where(low, t, swapped), jnp.where(low, -swapped, t)

    def rotate(u, cosine, sine):
        return (u * cosine + pltpu.roll(u, HEAD // 2, 1) * sine).astype(BF16)

    def term(d, start, size, weight):
        owner = lax.rem(me - d + n_rows, n_rows)
        return jnp.dot(
            xn[pl.ds(start, size), pl.ds(pl.multiple_of(owner * depth, depth), depth)],
            weight,
            preferred_element_type=F32,
        )

    def project(start, size, weight_of, before=lambda d: None):
        before(0)
        total = term(0, start, size, weight_of(0))
        for d in range(1, n_rows):
            before(d)
            total = total + term(d, start, size, weight_of(d))
        return total

    def ready_weight(i):
        def wait(d):
            if d == 0:
                own_copy(i).wait()
            else:
                weight_copy(d, i).wait_recv()

        return wait

    def store_keys(start, size, total):
        cosine, sine = tables(start, size)
        for h in range(kv_heads):
            cols = pl.ds(h * HEAD, HEAD)
            kbuf[pl.ds(mine + start, size), cols] = rotate(
                total[:, h * HEAD : (h + 1) * HEAD], cosine, sine
            )

    def store_values(start, size, total):
        vbuf[pl.ds(mine + start, size), :] = total.astype(BF16)

    high = rows - block
    for c in reversed(range(high // TQ, tiles)):
        norm(c)
    tab_copy.wait()
    total = project(high, block, lambda d: wkv_buf[d, :, pl.ds(0, kvw)], ready_weight(0))
    if paired:

        @pl.when(has_next & jnp.logical_not(first))
        def _():
            pl.semaphore_wait(barrier, 2)
            pl.semaphore_signal(ready, inc=1, device_id={"rows": 0}, device_id_type=MESH)

    store_keys(high, block, total)
    if paired:

        @pl.when(has_next & first)
        def _():
            pl.semaphore_wait(ready, 1)

    send([0])
    total = project(high, block, lambda d: wkv_buf[d, :, pl.ds(kvw, kvw)], ready_weight(1))
    store_values(high, block, total)
    send([1])
    sent = 2
    for b in reversed(range(high // block)):
        for c in reversed(range(block // TQ)):
            norm(b * (block // TQ) + c)
        total = project(b * block, block, lambda d: wkv_buf[d])
        store_keys(b * block, block, total[:, :kvw])
        store_values(b * block, block, total[:, kvw:])
        count = 2 * (block // TQ)
        send(range(sent, sent + count))
        sent += count

    for j in range(parts):
        total = project(0, rows, lambda d: wq_buf[j, d], ready_weight(2 + j))
        cosine, sine = tables(0, rows)
        for k in range(part // HEAD):
            h, g = divmod(j * (part // HEAD) + k, group)
            u = rotate(total[:, k * HEAD : (k + 1) * HEAD], cosine, sine)
            for t in range(tiles):
                q[t, h, pl.ds(g * TQ, TQ), :] = u[t * TQ : (t + 1) * TQ]
        relay(1)

    factor = math.log2(math.e) / math.sqrt(HEAD)

    def attend(t, s, lo, size, opens, closes):
        seen = s * rows + lo
        keys_at = pl.ds(seen, size)
        visible = jnp.tile(qdoc[pl.ds(t * TQ, TQ), :], (1, size // TQ)) == kdoc[:, keys_at]
        if s == back:
            query_at = lax.broadcasted_iota(jnp.int32, (TQ, 1), 0) + t * TQ
            key_at = lax.broadcasted_iota(jnp.int32, (1, size), 1) + lo
            visible = visible & (query_at >= key_at)
        for h in range(kv_heads):
            cols = pl.ds(h * HEAD, HEAD)
            scores = lax.dot_general(
                q[t, h], kbuf[keys_at, cols], (((1,), (1,)), ((), ())),
                preferred_element_type=F32,
            )
            scores = jnp.where(
                visible[None], scores.reshape(group, TQ, size), -1e30
            ).reshape(group * TQ, size)
            top = jnp.broadcast_to(
                jnp.max(scores, axis=-1, keepdims=True), (group * TQ, HEAD)
            )
            if not opens:
                older = tops[t, h]
                top = jnp.maximum(older, top)
                fade = jnp.exp2((older - top) * factor)
            weight = jnp.exp2((scores - jnp.tile(top, (1, size // HEAD))) * factor).astype(BF16)
            mixed = jnp.dot(
                weight,
                jnp.concatenate([vbuf[keys_at, cols], jnp.ones((size, HEAD), BF16)], axis=1),
                preferred_element_type=F32,
            )
            if not opens:
                mixed = acc[t, h] * jnp.tile(fade, (1, 2)) + mixed
            if closes:
                done = (mixed[:, :HEAD] / mixed[:, HEAD:]).astype(BF16)
                for g in range(group):
                    out[pl.ds(t * TQ, TQ), pl.ds((h * group + g) * HEAD, HEAD)] = done[
                        g * TQ : (g + 1) * TQ
                    ]
            else:
                acc[t, h] = mixed
                tops[t, h] = top

    def reach(t, s):
        return max(mine + (t + 1) * TQ - span - s * rows, 0)

    def final(t, s, lo):
        return lo <= reach(t, s) and all(reach(t, b) >= rows for b in range(s))

    for i, t in enumerate(reversed(range(tiles))):
        lo = reach(t, back)
        attend(t, back, lo, (t + 1) * TQ - lo, True, final(t, back, lo))
        if i % 2:
            relay(2)
    relay(len(relays))
    for s in reversed(range(1, back)):
        for t in reversed(range(tiles)):
            lo = reach(t, s)
            if lo < rows:
                attend(t, s, lo, rows - lo, False, final(t, s, lo))
    done = 0
    while done < len(last):
        for p in range(done, done + 2):
            arrived(*last[p])
        _, start, size = pieces[done]
        for t in reversed(range(tiles)):
            lo = max(reach(t, 0), start)
            if lo < start + size:
                attend(t, 0, lo, start + size - lo, False, final(t, 0, lo))
        done += 2

    for i in range(len(weights)):
        for d in range(1, n_rows):
            weight_copy(d, i).wait_send()
    for s in range(back):

        @pl.when((at >= s) & has_next)
        def _():
            for p in range(len(pieces)):
                hop(s, p).wait_send()


def solution(mesh):
    n_rows = mesh.shape["rows"]
    n_attn = mesh.shape["attn"]

    def on_device(tokens, norm_gain, w_query, w_key, w_value, documents):
        rows, width = tokens.shape
        depth, qw = w_query.shape
        kvw = w_key.shape[1]
        back = min(n_attn - 1, -(-(MOST - 1) // rows))
        block = 2 * TQ if rows % (2 * TQ) == 0 else rows
        part = 2 * HEAD if qw % (2 * HEAD) == 0 else qw
        pieces = 2 + 2 * ((rows - block) // TQ)
        table = jnp.asarray(rotary_table(documents.shape[1]))
        hbm = pl.BlockSpec(memory_space=pl.ANY)
        vmem = pl.BlockSpec(memory_space=pltpu.VMEM)
        keys = (back + 1) * rows
        group = qw // kvw
        heads = kvw // HEAD
        tiles = rows // TQ
        copies = 2 + qw // part
        args = (tokens, norm_gain, w_query, w_key, w_value, documents, table)
        return pl.pallas_call(
            functools.partial(kernel, n_rows, n_attn, back, block, part),
            out_shape=pltpu.VMEM((rows, qw), BF16),
            in_specs=[hbm, vmem, hbm, hbm, hbm, vmem, hbm],
            out_specs=vmem,
            scratch_shapes=[
                pltpu.VMEM((8, width), F32),
                pltpu.VMEM((rows, width), BF16),
                pltpu.VMEM((rows, width), BF16),
                pltpu.VMEM((n_rows, depth, 2 * kvw), BF16),
                pltpu.VMEM((qw // part, n_rows, depth, part), BF16),
                pltpu.VMEM((keys, kvw), BF16),
                pltpu.VMEM((keys, kvw), BF16),
                pltpu.VMEM((tiles, heads, group * TQ, HEAD), BF16),
                pltpu.VMEM((tiles, heads, group * TQ, HEAD), F32),
                pltpu.VMEM((tiles, heads, group * TQ, 2 * HEAD), F32),
                pltpu.VMEM((rows, HEAD), F32),
                pltpu.VMEM((1, keys), jnp.int32),
                pltpu.VMEM((rows, TQ), jnp.int32),
                pltpu.SemaphoreType.DMA((tiles,)),
                pltpu.SemaphoreType.DMA((copies + 1,)),
                pltpu.SemaphoreType.DMA((n_rows, copies)),
                pltpu.SemaphoreType.DMA((n_rows, copies)),
                pltpu.SemaphoreType.DMA((max(back, 1), pieces)),
                pltpu.SemaphoreType.DMA((max(back, 1), pieces)),
                pltpu.SemaphoreType.REGULAR,
            ],
            compiler_params=pltpu.CompilerParams(
                collective_id=0, has_side_effects=True, vmem_limit_bytes=48 << 20
            ),
            name="layer",
        )(*(pltpu.with_memory_space_constraint(a, pltpu.HBM) for a in args))

    placed = (
        P(("rows", "attn"), None),
        P(),
        P("rows", "tp"),
        P("rows", "tp"),
        P("rows", "tp"),
        P("rows", None),
    )
    return jax.shard_map(
        on_device, mesh=mesh, in_specs=placed, out_specs=P(("rows", "attn"), "tp"), check_vma=False
    )
```

time: 22.5 us -> 20 us (0.89)
  the two profiles are of different devices: /device:TPU:18 before, /device:TPU:0 now
where the time goes in v2:
time: 20 us; the launch traced here: 19.7 us
  Pallas kernels  18.9 us (94%)
  local copies, waits for them, and re-layouts  0.8 us (4%)
    pallas_call x1, Pallas kernels, on_device(): pl.pallas_call(functools.partial(kernel, n_rows, n_attn, back, block, par...  18.9 us
    unnamed x1, local copies, waits for them, and re-layouts  0.8 us

profile of v2, /device:TPU:0, one launch (start us, length us, event | category | flops | bytes accessed | tf_op | source)
XLA Modules:
  0.0 19.7 jit_solution(9740897178203291445)
XLA Ops:
  0.0 18.9 %layer.1 = bf16[512,512]{1,0:T(8,128)(2,1)S(1)} custom-call(bf16[512,4096]{1,0:T(8,128)(2,1)} %tok.1, bf16[4096]{0:T(1024)(128)(2,1)} %gain.1, bf16[2048,512]{1,0:T(8,128)(2,1)} %wq.1, bf16[2048,128]{1,0:T(8,128)(2,1)} %wk.1, bf16[2048,128]{1,0:T(8,128)(2,1)} %wv.1, s32[1,2048]{1,0:T(1,128)} %docs.1, f32[2048,128]{1,0:T(8,128)} %constant.2.clone.table), custom_call_target="tpu_custom_call" | custom-call | tf_op jit(solution)/shard_map/layer/pallas_call | solution.py:404
  18.9 0.8 %copy.9 = bf16[512,512]{1,0:T(8,128)(2,1)} copy(bf16[512,512]{1,0:T(8,128)(2,1)S(1)} %layer.1) | data formatting | bytes 1048576

commit v3 on v2

--- a/solution.py
+++ b/solution.py
@@ -27,9 +27,9 @@
 
 
 def kernel(
-    n_rows, n_attn, back, block, part,
-    tok, gain, wq, wk, wv, docs, table, out,
-    gains, xt, xn, wkv_buf, wq_buf, kbuf, vbuf, q, tops, acc, tab, kdoc, qdoc,
+    n_rows, n_attn, back, block, load,
+    tok, gain_in, wq, wk, wv, docs_in, table, out,
+    gain, docs, gains, xt, xn, wkv_buf, wq_buf, kbuf, vbuf, q, tops, acc, sums, qsum, tab, kdoc, qdoc,
     tok_sem, own_sem, w_send, w_recv, kv_send, kv_recv, ready,
 ):
     rows, width = tok.shape
@@ -37,7 +37,6 @@
     qw = wq.shape[1]
     kv_heads = kvw // HEAD
     group = qw // kvw
-    parts = qw // part
     tiles = rows // TQ
     mine = back * rows
     span = min(mine + rows, -(-(MOST - 1 + TQ) // TQ) * TQ)
@@ -47,14 +46,13 @@
     has_next = at < n_attn - 1
 
     def tok_copy(c):
-        here = pl.ds(c * TQ, TQ)
+        here = pl.ds(c * load, load)
         return pltpu.make_async_copy(tok.at[here], xt.at[here], tok_sem.at[c])
 
     weights = [
         (wk, lambda d: wkv_buf.at[d, :, pl.ds(0, kvw)]),
         (wv, lambda d: wkv_buf.at[d, :, pl.ds(kvw, kvw)]),
-    ] + [
-        (wq.at[:, pl.ds(j * part, part)], lambda d, j=j: wq_buf.at[j, d]) for j in range(parts)
+        (wq, lambda d: wq_buf.at[d]),
     ]
 
     def own_copy(i):
@@ -69,17 +67,26 @@
             device_id={"rows": lax.rem(me + d, n_rows)}, device_id_type=MESH,
         )
 
+    small = [
+        pltpu.make_async_copy(src, dst, own_sem.at[len(weights) + 1 + i])
+        for i, (src, dst) in enumerate(((gain_in, gain), (docs_in, docs)))
+    ]
     tab_copy = pltpu.make_async_copy(
         table.at[pl.ds(pl.multiple_of(at * rows, rows), rows)], tab, own_sem.at[len(weights)]
     )
 
-    tok_copy(tiles - 1).start()
+    loads = rows // load
+    early = max(loads - block // load, 1)
+    small[0].start()
+    tok_copy(loads - 1).start()
+    small[1].start()
     own_copy(0).start()
-    for c in reversed(range(tiles - 1)):
+    for c in reversed(range(early, loads - 1)):
         tok_copy(c).start()
-        if c == tiles - 2:
-            tab_copy.start()
-            own_copy(1).start()
+    tab_copy.start()
+    own_copy(1).start()
+    for c in reversed(range(min(early, loads - 1))):
+        tok_copy(c).start()
 
     barrier = pltpu.get_barrier_semaphore()
     paired = n_rows == 2 and n_attn > 1
@@ -129,6 +136,7 @@
     for i in range(2, len(weights)):
         own_copy(i).start()
 
+    small[1].wait()
     for s in range(back + 1):
         owner = at - back + s
         keep = pl.multiple_of(jnp.maximum(owner, 0) * rows, rows)
@@ -143,6 +151,7 @@
             kbuf[pl.ds(s * rows, rows), :] = jnp.zeros((rows, kvw), BF16)
             vbuf[pl.ds(s * rows, rows), :] = jnp.zeros((rows, kvw), BF16)
 
+    small[0].wait()
     gains[...] = jnp.broadcast_to(gain[...].astype(F32).reshape(1, -1), gains.shape)
 
     pieces = [(which, rows - block, block) for which in range(2)]
@@ -188,11 +197,9 @@
     strip, piece = 16, 256
 
     def norm(c):
-        tok_copy(c).wait()
-
-        @pl.loop(0, TQ // strip, unroll=4)
+        @pl.loop(0, load // strip, unroll=4)
         def _(i):
-            here = pl.ds(pl.multiple_of(c * TQ + i * strip, strip), strip)
+            here = pl.ds(pl.multiple_of(c * load + i * strip, strip), strip)
             squares = jnp.zeros((strip, piece), F32)
             for k in range(width // piece):
                 x = xt[here, pl.ds(k * piece, piece)].astype(F32)
@@ -217,30 +224,29 @@
     def rotate(u, cosine, sine):
         return (u * cosine + pltpu.roll(u, HEAD // 2, 1) * sine).astype(BF16)
 
-    def term(d, start, size, weight):
-        owner = lax.rem(me - d + n_rows, n_rows)
-        return jnp.dot(
-            xn[pl.ds(start, size), pl.ds(pl.multiple_of(owner * depth, depth), depth)],
-            weight,
-            preferred_element_type=F32,
-        )
-
-    def project(start, size, weight_of, before=lambda d: None):
-        before(0)
-        total = term(0, start, size, weight_of(0))
-        for d in range(1, n_rows):
-            before(d)
-            total = total + term(d, start, size, weight_of(d))
+    half = depth // 2 if depth % (2 * HEAD) == 0 else depth
+
+    def dots(start, size, terms, weight):
+        total = None
+        for d, k in terms:
+            owner = lax.rem(me - d + n_rows, n_rows)
+            here = pl.ds(pl.multiple_of(owner * depth + k, half), half)
+            term = jnp.dot(
+                xn[pl.ds(start, size), here], weight(d, k), preferred_element_type=F32
+            )
+            total = term if total is None else total + term
         return total
 
-    def ready_weight(i):
-        def wait(d):
-            if d == 0:
-                own_copy(i).wait()
-            else:
-                weight_copy(d, i).wait_recv()
-
-        return wait
+    def project(start, size, first_col, cols):
+        def weight(d, k):
+            return wkv_buf[d, pl.ds(k, half), pl.ds(first_col, cols)]
+
+        terms = [(d, k) for d in range(n_rows) for k in range(0, depth, half)]
+        for chain in range(2):
+            sums[chain, pl.ds(0, size), pl.ds(0, cols)] = dots(
+                start, size, terms[chain::2], weight
+            )
+        return sums[0, pl.ds(0, size), pl.ds(0, cols)] + sums[1, pl.ds(0, size), pl.ds(0, cols)]
 
     def store_keys(start, size, total):
         cosine, sine = tables(start, size)
@@ -254,10 +260,18 @@
         vbuf[pl.ds(mine + start, size), :] = total.astype(BF16)
 
     high = rows - block
-    for c in reversed(range(high // TQ, tiles)):
+    for c in reversed(range(high // load, loads)):
+        tok_copy(c).wait()
         norm(c)
     tab_copy.wait()
-    total = project(high, block, lambda d: wkv_buf[d, :, pl.ds(0, kvw)], ready_weight(0))
+
+    def weight_ready(i):
+        own_copy(i).wait()
+        for d in range(1, n_rows):
+            weight_copy(d, i).wait_recv()
+
+    weight_ready(0)
+    total = project(high, block, 0, kvw)
     if paired:
 
         @pl.when(has_next & jnp.logical_not(first))
@@ -273,29 +287,46 @@
             pl.semaphore_wait(ready, 1)
 
     send([0])
-    total = project(high, block, lambda d: wkv_buf[d, :, pl.ds(kvw, kvw)], ready_weight(1))
-    store_values(high, block, total)
+    for c in reversed(range(high // load)):
+        tok_copy(c).wait()
+    weight_ready(1)
+    store_values(high, block, project(high, block, kvw, kvw))
+    for c in reversed(range(high // load)):
+        norm(c)
     send([1])
     sent = 2
     for b in reversed(range(high // block)):
-        for c in reversed(range(block // TQ)):
-            norm(b * (block // TQ) + c)
-        total = project(b * block, block, lambda d: wkv_buf[d])
+        total = project(b * block, block, 0, 2 * kvw)
         store_keys(b * block, block, total[:, :kvw])
         store_values(b * block, block, total[:, kvw:])
         count = 2 * (block // TQ)
         send(range(sent, sent + count))
         sent += count
 
-    for j in range(parts):
-        total = project(0, rows, lambda d: wq_buf[j, d], ready_weight(2 + j))
-        cosine, sine = tables(0, rows)
-        for k in range(part // HEAD):
-            h, g = divmod(j * (part // HEAD) + k, group)
-            u = rotate(total[:, k * HEAD : (k + 1) * HEAD], cosine, sine)
-            for t in range(tiles):
-                q[t, h, pl.ds(g * TQ, TQ), :] = u[t * TQ : (t + 1) * TQ]
-        relay(1)
+    def queries(start, d):
+        owner = lax.rem(me - d + n_rows, n_rows)
+        here = pl.ds(pl.multiple_of(owner * depth, depth), depth)
+        return jnp.dot(xn[pl.ds(start, block), here], wq_buf[d], preferred_element_type=F32)
+
+    steps = [b * block for b in reversed(range(rows // block))]
+    own_copy(2).wait()
+    for start in steps:
+        qsum[pl.ds(start, block), :] = queries(start, 0)
+    relay(1)
+    for d in range(1, n_rows):
+        weight_copy(d, 2).wait_recv()
+    for start in steps:
+        total = qsum[pl.ds(start, block), :]
+        for d in range(1, n_rows):
+            total = total + queries(start, d)
+        cosine, sine = tables(start, block)
+        for h in range(kv_heads):
+            for g in range(group):
+                col = (h * group + g) * HEAD
+                u = rotate(total[:, col : col + HEAD], cosine, sine)
+                for t in range(block // TQ):
+                    q[start // TQ + t, h, pl.ds(g * TQ, TQ), :] = u[t * TQ : (t + 1) * TQ]
+    relay(1)
 
     factor = math.log2(math.e) / math.sqrt(HEAD)
 
@@ -358,8 +389,19 @@
             lo = reach(t, s)
             if lo < rows:
                 attend(t, s, lo, rows - lo, False, final(t, s, lo))
+    for i in range(len(weights)):
+        for d in range(1, n_rows):
+            weight_copy(d, i).wait_send()
     done = 0
     while done < len(last):
+        if done + 2 >= len(last):
+            for s in range(back):
+
+                @pl.when((at >= s) & has_next)
+                def _():
+                    for p in range(len(pieces)):
+                        hop(s, p).wait_send()
+
         for p in range(done, done + 2):
             arrived(*last[p])
         _, start, size = pieces[done]
@@ -369,16 +411,6 @@
                 attend(t, 0, lo, start + size - lo, False, final(t, 0, lo))
         done += 2
 
-    for i in range(len(weights)):
-        for d in range(1, n_rows):
-            weight_copy(d, i).wait_send()
-    for s in range(back):
-
-        @pl.when((at >= s) & has_next)
-        def _():
-            for p in range(len(pieces)):
-                hop(s, p).wait_send()
-
 
 def solution(mesh):
     n_rows = mesh.shape["rows"]
@@ -390,7 +422,7 @@
         kvw = w_key.shape[1]
         back = min(n_attn - 1, -(-(MOST - 1) // rows))
         block = 2 * TQ if rows % (2 * TQ) == 0 else rows
-        part = 2 * HEAD if qw % (2 * HEAD) == 0 else qw
+        load = TQ // 2
         pieces = 2 + 2 * ((rows - block) // TQ)
         table = jnp.asarray(rotary_table(documents.shape[1]))
         hbm = pl.BlockSpec(memory_space=pl.ANY)
@@ -399,29 +431,33 @@
         group = qw // kvw
         heads = kvw // HEAD
         tiles = rows // TQ
-        copies = 2 + qw // part
+        copies = 3
         args = (tokens, norm_gain, w_query, w_key, w_value, documents, table)
         return pl.pallas_call(
-            functools.partial(kernel, n_rows, n_attn, back, block, part),
+            functools.partial(kernel, n_rows, n_attn, back, block, load),
             out_shape=pltpu.VMEM((rows, qw), BF16),
-            in_specs=[hbm, vmem, hbm, hbm, hbm, vmem, hbm],
+            in_specs=[hbm] * len(args),
             out_specs=vmem,
             scratch_shapes=[
+                pltpu.VMEM((width,), BF16),
+                pltpu.VMEM(documents.shape, jnp.int32),
                 pltpu.VMEM((8, width), F32),
                 pltpu.VMEM((rows, width), BF16),
                 pltpu.VMEM((rows, width), BF16),
                 pltpu.VMEM((n_rows, depth, 2 * kvw), BF16),
-                pltpu.VMEM((qw // part, n_rows, depth, part), BF16),
+                pltpu.VMEM((n_rows, depth, qw), BF16),
                 pltpu.VMEM((keys, kvw), BF16),
                 pltpu.VMEM((keys, kvw), BF16),
                 pltpu.VMEM((tiles, heads, group * TQ, HEAD), BF16),
                 pltpu.VMEM((tiles, heads, group * TQ, HEAD), F32),
                 pltpu.VMEM((tiles, heads, group * TQ, 2 * HEAD), F32),
+                pltpu.VMEM((2, block, 2 * kvw), F32),
+                pltpu.VMEM((rows, qw), F32),
                 pltpu.VMEM((rows, HEAD), F32),
                 pltpu.VMEM((1, keys), jnp.int32),
                 pltpu.VMEM((rows, TQ), jnp.int32),
-                pltpu.SemaphoreType.DMA((tiles,)),
-                pltpu.SemaphoreType.DMA((copies + 1,)),
+                pltpu.SemaphoreType.DMA((rows // load,)),
+                pltpu.SemaphoreType.DMA((copies + 3,)),
                 pltpu.SemaphoreType.DMA((n_rows, copies)),
                 pltpu.SemaphoreType.DMA((n_rows, copies)),
                 pltpu.SemaphoreType.DMA((max(back, 1), pieces)),

time: 20 us -> 17.8 us (0.89)
  the two profiles are of different devices: /device:TPU:0 before, /device:TPU:18 now
where the time goes in v3:
time: 17.8 us; the launch traced here: 17.6 us
  Pallas kernels  16.8 us (94%)
  local copies, waits for them, and re-layouts  0.8 us (4%)
    pallas_call x1, Pallas kernels, on_device(): pl.pallas_call(functools.partial(kernel, n_rows, n_attn, back, block, loa...  16.8 us
    unnamed x1, local copies, waits for them, and re-layouts  0.8 us

profile of v3, /device:TPU:18, one launch (start us, length us, event | category | flops | bytes accessed | tf_op | source)
XLA Modules:
  0.0 17.6 jit_solution(7048028470372872853)
XLA Ops:
  0.0 16.8 %layer.1 = bf16[512,512]{1,0:T(8,128)(2,1)S(1)} custom-call(bf16[512,4096]{1,0:T(8,128)(2,1)} %tok.1, bf16[4096]{0:T(1024)(128)(2,1)} %gain_in.1, bf16[2048,512]{1,0:T(8,128)(2,1)} %wq.1, bf16[2048,128]{1,0:T(8,128)(2,1)} %wk.1, bf16[2048,128]{1,0:T(8,128)(2,1)} %wv.1, s32[1,2048]{1,0:T(1,128)} %docs_in.1, f32[2048,128]{1,0:T(8,128)} %constant.2.clone.table), custom_call_target="tpu_custom_call" | custom-call | tf_op jit(solution)/shard_map/layer/pallas_call | solution.py:436
  16.8 0.8 %copy.9 = bf16[512,512]{1,0:T(8,128)(2,1)} copy(bf16[512,512]{1,0:T(8,128)(2,1)S(1)} %layer.1) | data formatting | bytes 1048576

commit v4 on v3

--- a/solution.py
+++ b/solution.py
@@ -76,17 +76,13 @@
     )
 
     loads = rows // load
-    early = max(loads - block // load, 1)
+    early = loads - block // load
     small[0].start()
-    tok_copy(loads - 1).start()
-    small[1].start()
-    own_copy(0).start()
-    for c in reversed(range(early, loads - 1)):
+    for c in reversed(range(early, loads)):
         tok_copy(c).start()
+        if c == max(loads - 2, early):
+            own_copy(0).start()
     tab_copy.start()
-    own_copy(1).start()
-    for c in reversed(range(min(early, loads - 1))):
-        tok_copy(c).start()
 
     barrier = pltpu.get_barrier_semaphore()
     paired = n_rows == 2 and n_attn > 1
@@ -122,7 +118,7 @@
         elif n_rows > 1:
             pl.semaphore_wait(barrier, n_rows - 1)
 
-    for i in range(len(weights)):
+    for i in range(2):
         for d in range(1, n_rows):
             weight_copy(d, i).start()
     if paired:
@@ -133,17 +129,6 @@
                 barrier, inc=1, device_id={"rows": 1, "attn": at - 1}, device_id_type=MESH
             )
 
-    for i in range(2, len(weights)):
-        own_copy(i).start()
-
-    small[1].wait()
-    for s in range(back + 1):
-        owner = at - back + s
-        keep = pl.multiple_of(jnp.maximum(owner, 0) * rows, rows)
-        kdoc[:, pl.ds(s * rows, rows)] = jnp.where(owner >= 0, docs[:, pl.ds(keep, rows)], -1)
-    for t in range(tiles):
-        row = kdoc[:, pl.ds(mine + t * TQ, TQ)]
-        qdoc[pl.ds(t * TQ, TQ), :] = jnp.broadcast_to(row, (TQ, TQ)).T
     for s in range(back):
 
         @pl.when(at - back + s < 0)
@@ -151,12 +136,13 @@
             kbuf[pl.ds(s * rows, rows), :] = jnp.zeros((rows, kvw), BF16)
             vbuf[pl.ds(s * rows, rows), :] = jnp.zeros((rows, kvw), BF16)
 
-    small[0].wait()
-    gains[...] = jnp.broadcast_to(gain[...].astype(F32).reshape(1, -1), gains.shape)
-
-    pieces = [(which, rows - block, block) for which in range(2)]
-    for c in reversed(range((rows - block) // TQ)):
-        pieces += [(which, c * TQ, TQ) for which in range(2)]
+    upper = block // TQ
+    pieces = [
+        (which, c * TQ, TQ)
+        for b in reversed(range(rows // block))
+        for which in range(2)
+        for c in reversed(range(b * upper, (b + 1) * upper))
+    ]
 
     def hop(s, p):
         which, start, size = pieces[p]
@@ -260,48 +246,94 @@
         vbuf[pl.ds(mine + start, size), :] = total.astype(BF16)
 
     high = rows - block
-    for c in reversed(range(high // load, loads)):
-        tok_copy(c).wait()
-        norm(c)
-    tab_copy.wait()
+    per = TQ // load
+
+    def norm_chunk(c):
+        for i in reversed(range(c * per, (c + 1) * per)):
+            norm(i)
+
+    def tok_wait(c):
+        for i in reversed(range(c * per, (c + 1) * per)):
+            tok_copy(i).wait()
 
     def weight_ready(i):
-        own_copy(i).wait()
         for d in range(1, n_rows):
             weight_copy(d, i).wait_recv()
 
+    for c in reversed(range(high // TQ, tiles)):
+        tok_wait(c)
+        if c == tiles - 1:
+            small[0].wait()
+            gains[...] = jnp.broadcast_to(gain[...].astype(F32).reshape(1, -1), gains.shape)
+        norm_chunk(c)
+        if c == tiles - 1:
+            own_copy(1).start()
+            for i in reversed(range(early)):
+                tok_copy(i).start()
+            for d in range(1, n_rows):
+                weight_copy(d, 2).start()
+            small[1].start()
+            own_copy(2).start()
+    tab_copy.wait()
+    own_copy(0).wait()
+    key_cols = pl.ds(0, kvw)
+
+    def key_weight(d, k):
+        return wkv_buf[d, pl.ds(k, half), key_cols]
+
+    own = [(0, k) for k in range(0, depth, half)]
+    for chain in range(2):
+        sums[chain, :, key_cols] = (
+            dots(high, block, own[chain::2], key_weight)
+            if own[chain::2]
+            else jnp.zeros((block, kvw), F32)
+        )
     weight_ready(0)
-    total = project(high, block, 0, kvw)
-    if paired:
-
-        @pl.when(has_next & jnp.logical_not(first))
-        def _():
-            pl.semaphore_wait(barrier, 2)
-            pl.semaphore_signal(ready, inc=1, device_id={"rows": 0}, device_id_type=MESH)
-
-    store_keys(high, block, total)
-    if paired:
-
-        @pl.when(has_next & first)
-        def _():
-            pl.semaphore_wait(ready, 1)
-
-    send([0])
-    for c in reversed(range(high // load)):
-        tok_copy(c).wait()
+    far = [(d, k) for d in range(1, n_rows) for k in range(0, depth, half)]
+    for i in range(upper):
+        start = rows - (i + 1) * TQ
+        here = pl.ds(start - high, TQ)
+        for chain in range(2):
+            if far[chain::2]:
+                sums[chain, here, key_cols] = sums[chain, here, key_cols] + dots(
+                    start, TQ, far[chain::2], key_weight
+                )
+        store_keys(start, TQ, sums[0, here, key_cols] + sums[1, here, key_cols])
+        if i == 0 and paired:
+
+            @pl.when(has_next & jnp.logical_not(first))
+            def _():
+                pl.semaphore_wait(barrier, 2)
+                pl.semaphore_signal(ready, inc=1, device_id={"rows": 0}, device_id_type=MESH)
+
+            @pl.when(has_next & first)
+            def _():
+                pl.semaphore_wait(ready, 1)
+
+        send([i])
+    own_copy(1).wait()
     weight_ready(1)
     store_values(high, block, project(high, block, kvw, kvw))
-    for c in reversed(range(high // load)):
-        norm(c)
-    send([1])
-    sent = 2
+    send(range(upper, 2 * upper))
+    for c in reversed(range(high // TQ)):
+        tok_wait(c)
+    for c in reversed(range(high // TQ)):
+        norm_chunk(c)
+    sent = 2 * upper
     for b in reversed(range(high // block)):
-        total = project(b * block, block, 0, 2 * kvw)
-        store_keys(b * block, block, total[:, :kvw])
-        store_values(b * block, block, total[:, kvw:])
-        count = 2 * (block // TQ)
-        send(range(sent, sent + count))
-        sent += count
+        store_keys(b * block, block, project(b * block, block, 0, kvw))
+        send(range(sent, sent + upper))
+        store_values(b * block, block, project(b * block, block, kvw, kvw))
+        send(range(sent + upper, sent + 2 * upper))
+        sent += 2 * upper
+    small[1].wait()
+    for s in range(back + 1):
+        owner = at - back + s
+        keep = pl.multiple_of(jnp.maximum(owner, 0) * rows, rows)
+        kdoc[:, pl.ds(s * rows, rows)] = jnp.where(owner >= 0, docs[:, pl.ds(keep, rows)], -1)
+    for t in range(tiles):
+        row = kdoc[:, pl.ds(mine + t * TQ, TQ)]
+        qdoc[pl.ds(t * TQ, TQ), :] = jnp.broadcast_to(row, (TQ, TQ)).T
 
     def queries(start, d):
         owner = lax.rem(me - d + n_rows, n_rows)
@@ -312,7 +344,7 @@
     own_copy(2).wait()
     for start in steps:
         qsum[pl.ds(start, block), :] = queries(start, 0)
-    relay(1)
+    relay(2)
     for d in range(1, n_rows):
         weight_copy(d, 2).wait_recv()
     for start in steps:
@@ -326,11 +358,11 @@
                 u = rotate(total[:, col : col + HEAD], cosine, sine)
                 for t in range(block // TQ):
                     q[start // TQ + t, h, pl.ds(g * TQ, TQ), :] = u[t * TQ : (t + 1) * TQ]
-    relay(1)
+    relay(2)
 
     factor = math.log2(math.e) / math.sqrt(HEAD)
 
-    def attend(t, s, lo, size, opens, closes):
+    def weigh(t, s, lo, size, opens):
         seen = s * rows + lo
         keys_at = pl.ds(seen, size)
         visible = jnp.tile(qdoc[pl.ds(t * TQ, TQ), :], (1, size // TQ)) == kdoc[:, keys_at]
@@ -338,10 +370,10 @@
             query_at = lax.broadcasted_iota(jnp.int32, (TQ, 1), 0) + t * TQ
             key_at = lax.broadcasted_iota(jnp.int32, (1, size), 1) + lo
             visible = visible & (query_at >= key_at)
+        made = []
         for h in range(kv_heads):
-            cols = pl.ds(h * HEAD, HEAD)
             scores = lax.dot_general(
-                q[t, h], kbuf[keys_at, cols], (((1,), (1,)), ((), ())),
+                q[t, h], kbuf[keys_at, pl.ds(h * HEAD, HEAD)], (((1,), (1,)), ((), ())),
                 preferred_element_type=F32,
             )
             scores = jnp.where(
@@ -350,17 +382,28 @@
             top = jnp.broadcast_to(
                 jnp.max(scores, axis=-1, keepdims=True), (group * TQ, HEAD)
             )
+            fade = None
             if not opens:
                 older = tops[t, h]
                 top = jnp.maximum(older, top)
                 fade = jnp.exp2((older - top) * factor)
             weight = jnp.exp2((scores - jnp.tile(top, (1, size // HEAD))) * factor).astype(BF16)
+            made.append((weight, fade))
+            tops[t, h] = top
+        return made
+
+    def mix(t, s, lo, size, made, closes):
+        keys_at = pl.ds(s * rows + lo, size)
+        for h in range(kv_heads):
+            weight, fade = made[h]
             mixed = jnp.dot(
                 weight,
-                jnp.concatenate([vbuf[keys_at, cols], jnp.ones((size, HEAD), BF16)], axis=1),
+                jnp.concatenate(
+                    [vbuf[keys_at, pl.ds(h * HEAD, HEAD)], jnp.ones((size, HEAD), BF16)], axis=1
+                ),
                 preferred_element_type=F32,
             )
-            if not opens:
+            if fade is not None:
                 mixed = acc[t, h] * jnp.tile(fade, (1, 2)) + mixed
             if closes:
                 done = (mixed[:, :HEAD] / mixed[:, HEAD:]).astype(BF16)
@@ -370,7 +413,9 @@
                     ]
             else:
                 acc[t, h] = mixed
-                tops[t, h] = top
+
+    def attend(t, s, lo, size, opens, closes):
+        mix(t, s, lo, size, weigh(t, s, lo, size, opens), closes)
 
     def reach(t, s):
         return max(mine + (t + 1) * TQ - span - s * rows, 0)
@@ -392,24 +437,74 @@
     for i in range(len(weights)):
         for d in range(1, n_rows):
             weight_copy(d, i).wait_send()
-    done = 0
-    while done < len(last):
-        if done + 2 >= len(last):
-            for s in range(back):
-
-                @pl.when((at >= s) & has_next)
-                def _():
-                    for p in range(len(pieces)):
-                        hop(s, p).wait_send()
-
-        for p in range(done, done + 2):
-            arrived(*last[p])
-        _, start, size = pieces[done]
-        for t in reversed(range(tiles)):
-            lo = max(reach(t, 0), start)
-            if lo < start + size:
-                attend(t, 0, lo, start + size - lo, False, final(t, 0, lo))
-        done += 2
+    def come(which, start, size):
+        for s, p in last:
+            if pieces[p][0] == which and start <= pieces[p][1] < start + size:
+                arrived(s, p)
+
+    def sent_all():
+        for s in range(back):
+
+            @pl.when((at >= s) & has_next)
+            def _():
+                for p in range(len(pieces)):
+                    hop(s, p).wait_send()
+
+    blocks = list(reversed(range(0, rows, block))) if back else []
+    for start in blocks:
+        end = start + block
+        low = {t: max(reach(t, 0), start) for t in reversed(range(tiles))}
+        low = {t: lo for t, lo in low.items() if lo < end}
+        if start == high and start > 0:
+            come(0, start, block)
+            made = {t: weigh(t, 0, lo, end - lo, False) for t, lo in low.items()}
+            come(1, start, block)
+            for t, lo in low.items():
+                mix(t, 0, lo, end - lo, made[t], final(t, 0, lo))
+            continue
+        pairs = [(t, h) for t in low for h in range(kv_heads)]
+        base = {(t, h): acc[t, h][:, :HEAD] for t, h in pairs}
+        total = {(t, h): acc[t, h][:, HEAD:] for t, h in pairs}
+        made = {}
+        for c in reversed(range(start, end, TQ)):
+            come(0, c, TQ)
+            for t, lo in low.items():
+                if lo > c:
+                    continue
+                for h, (weight, fade) in enumerate(weigh(t, 0, c, TQ, False)):
+                    for e in range(c + TQ, end, TQ):
+                        older, carry = made[t, h, e]
+                        made[t, h, e] = older, fade if carry is None else carry * fade
+                    made[t, h, c] = weight, None
+                    base[t, h] = base[t, h] * fade
+                    total[t, h] = total[t, h] * fade + jnp.dot(
+                        weight, jnp.ones((TQ, HEAD), BF16), preferred_element_type=F32
+                    )
+                    if c == lo and final(t, 0, lo):
+                        total[t, h] = 1.0 / total[t, h]
+        for c in reversed(range(start, end, TQ)):
+            if c == 0:
+                sent_all()
+            come(1, c, TQ)
+            for t, h in pairs:
+                if low[t] > c:
+                    continue
+                weight, carry = made[t, h, c]
+                fresh = jnp.dot(
+                    weight, vbuf[pl.ds(c, TQ), pl.ds(h * HEAD, HEAD)],
+                    preferred_element_type=F32,
+                )
+                base[t, h] = base[t, h] + (fresh if carry is None else fresh * carry)
+                if low[t] < c:
+                    continue
+                if final(t, 0, low[t]):
+                    done = (base[t, h] * total[t, h]).astype(BF16)
+                    for g in range(group):
+                        out[pl.ds(t * TQ, TQ), pl.ds((h * group + g) * HEAD, HEAD)] = done[
+                            g * TQ : (g + 1) * TQ
+                        ]
+                else:
+                    acc[t, h] = jnp.concatenate([base[t, h], total[t, h]], axis=1)
 
 
 def solution(mesh):
@@ -423,7 +518,7 @@
         back = min(n_attn - 1, -(-(MOST - 1) // rows))
         block = 2 * TQ if rows % (2 * TQ) == 0 else rows
         load = TQ // 2
-        pieces = 2 + 2 * ((rows - block) // TQ)
+        pieces = 2 * (rows // TQ)
         table = jnp.asarray(rotary_table(documents.shape[1]))
         hbm = pl.BlockSpec(memory_space=pl.ANY)
         vmem = pl.BlockSpec(memory_space=pltpu.VMEM)

time: 17.8 us -> 17 us (0.955)
  Pallas kernels: 16.8 us -> 16.1 us
    pallas_call x1, Pallas kernels: 16.8 us -> 16.1 us  [on_device(): pl.pallas_call(functools.partial(kernel, n_rows, n_attn, back, block, loa...]
where the time goes in v4:
time: 17 us; the launch traced here: 16.9 us
  Pallas kernels  16.1 us (95%)
  local copies, waits for them, and re-layouts  0.8 us (5%)
    pallas_call x1, Pallas kernels, on_device(): pl.pallas_call(functools.partial(kernel, n_rows, n_attn, back, block, loa...  16.1 us
    unnamed x1, local copies, waits for them, and re-layouts  0.8 us

profile of v4, /device:TPU:18, one launch (start us, length us, event | category | flops | bytes accessed | tf_op | source)
XLA Modules:
  0.0 16.9 jit_solution(9241666794051610537)
XLA Ops:
  0.0 16.1 %layer.1 = bf16[512,512]{1,0:T(8,128)(2,1)S(1)} custom-call(bf16[512,4096]{1,0:T(8,128)(2,1)} %tok.1, bf16[4096]{0:T(1024)(128)(2,1)} %gain_in.1, bf16[2048,512]{1,0:T(8,128)(2,1)} %wq.1, bf16[2048,128]{1,0:T(8,128)(2,1)} %wk.1, bf16[2048,128]{1,0:T(8,128)(2,1)} %wv.1, s32[1,2048]{1,0:T(1,128)} %docs_in.1, f32[2048,128]{1,0:T(8,128)} %constant.2.clone.table), custom_call_target="tpu_custom_call" | custom-call | tf_op jit(solution)/shard_map/layer/pallas_call | solution.py:531
  16.1 0.8 %copy.9 = bf16[512,512]{1,0:T(8,128)(2,1)} copy(bf16[512,512]{1,0:T(8,128)(2,1)S(1)} %layer.1) | data formatting | bytes 1048576

commit v5 on v4

--- a/solution.py
+++ b/solution.py
@@ -26,11 +26,26 @@
     return np.concatenate([np.cos(angles), np.sin(angles)], axis=1).astype(np.float32)
 
 
+def hop_copies(rows, block, back):
+    copies = []
+    for s in range(back):
+        unit = 0
+        for b in reversed(range(rows // block)):
+            for which in range(2):
+                upper = b == rows // block - 1
+                fine = (upper and which == 0) if s == 0 else (s == back - 1 and not upper)
+                size = TQ if fine else block
+                for start in reversed(range(b * block, (b + 1) * block, size)):
+                    copies.append((s, unit, which, start, size))
+                unit += 1
+    return copies
+
+
 def kernel(
-    n_rows, n_attn, back, block, load,
+    n_rows, n_attn, back, block,
     tok, gain_in, wq, wk, wv, docs_in, table, out,
     gain, docs, gains, xt, xn, wkv_buf, wq_buf, kbuf, vbuf, q, tops, acc, sums, qsum, tab, kdoc, qdoc,
-    tok_sem, own_sem, w_send, w_recv, kv_send, kv_recv, ready,
+    own_sem, w_send, w_recv, kv_send, kv_recv, ready,
 ):
     rows, width = tok.shape
     depth, kvw = wk.shape
@@ -45,9 +60,16 @@
     has_prev = at > 0
     has_next = at < n_attn - 1
 
-    def tok_copy(c):
-        here = pl.ds(c * load, load)
-        return pltpu.make_async_copy(tok.at[here], xt.at[here], tok_sem.at[c])
+    high = rows - block
+    top = rows - TQ
+    tok_parts = [(top + TQ // 2, TQ // 2, 2), (top, TQ // 2, 1)]
+    tok_parts += [(c, TQ, 6 + i) for i, c in enumerate(reversed(range(high, top, TQ)))]
+    tok_parts += [(0, high, 2)] if high else []
+
+    def tok_copy(i):
+        start, size, slot = tok_parts[i]
+        here = pl.ds(start, size)
+        return pltpu.make_async_copy(tok.at[here], xt.at[here], own_sem.at[slot])
 
     weights = [
         (wk, lambda d: wkv_buf.at[d, :, pl.ds(0, kvw)]),
@@ -57,31 +79,31 @@
 
     def own_copy(i):
         src, dst = weights[i]
-        return pltpu.make_async_copy(src, dst(0), own_sem.at[i])
+        return pltpu.make_async_copy(src, dst(0), own_sem.at[(3, 0, 5)[i]])
 
     def weight_copy(d, i):
         src, dst = weights[i]
         return pltpu.make_async_remote_copy(
             src_ref=src, dst_ref=dst(d),
-            send_sem=w_send.at[d, i], recv_sem=w_recv.at[d, i],
+            send_sem=w_send.at[d - 1, i], recv_sem=w_recv.at[d - 1, i],
             device_id={"rows": lax.rem(me + d, n_rows)}, device_id_type=MESH,
         )
 
     small = [
-        pltpu.make_async_copy(src, dst, own_sem.at[len(weights) + 1 + i])
+        pltpu.make_async_copy(src, dst, own_sem.at[i])
         for i, (src, dst) in enumerate(((gain_in, gain), (docs_in, docs)))
     ]
     tab_copy = pltpu.make_async_copy(
-        table.at[pl.ds(pl.multiple_of(at * rows, rows), rows)], tab, own_sem.at[len(weights)]
+        table.at[pl.ds(pl.multiple_of(at * rows, rows), rows)], tab, own_sem.at[4]
     )
 
-    loads = rows // load
-    early = loads - block // load
     small[0].start()
-    for c in reversed(range(early, loads)):
-        tok_copy(c).start()
-        if c == max(loads - 2, early):
-            own_copy(0).start()
+    tok_copy(0).start()
+    tok_copy(1).start()
+    own_copy(0).start()
+    near = range(2, 2 + (top - high) // TQ)
+    for i in near:
+        tok_copy(i).start()
     tab_copy.start()
 
     barrier = pltpu.get_barrier_semaphore()
@@ -136,56 +158,61 @@
             kbuf[pl.ds(s * rows, rows), :] = jnp.zeros((rows, kvw), BF16)
             vbuf[pl.ds(s * rows, rows), :] = jnp.zeros((rows, kvw), BF16)
 
-    upper = block // TQ
-    pieces = [
-        (which, c * TQ, TQ)
-        for b in reversed(range(rows // block))
-        for which in range(2)
-        for c in reversed(range(b * upper, (b + 1) * upper))
-    ]
-
-    def hop(s, p):
-        which, start, size = pieces[p]
+    copies = hop_copies(rows, block, back)
+
+    def hop(p):
+        s, _, which, start, size = copies[p]
         ref = (kbuf, vbuf)[which]
         return pltpu.make_async_remote_copy(
             src_ref=ref.at[pl.ds((back - s) * rows + start, size)],
             dst_ref=ref.at[pl.ds((back - s - 1) * rows + start, size)],
-            send_sem=kv_send.at[s, p], recv_sem=kv_recv.at[s, p],
+            send_sem=kv_send.at[s], recv_sem=kv_recv.at[p],
             device_id={"attn": jnp.minimum(at + 1, n_attn - 1)}, device_id_type=MESH,
         )
 
-    def send(wanted):
+    def all_sent(s):
+        ref = kbuf.at[pl.ds(0, 2 * rows)]
+        pltpu.make_async_remote_copy(
+            src_ref=ref, dst_ref=ref, send_sem=kv_send.at[s], recv_sem=kv_recv.at[0],
+            device_id={"attn": jnp.minimum(at + 1, n_attn - 1)}, device_id_type=MESH,
+        ).wait_send()
+
+    def send(which, start, size):
         if back:
 
             @pl.when(has_next)
             def _():
+                for p, (s, _, kind, row, _) in enumerate(copies):
+                    if s == 0 and kind == which and start <= row < start + size:
+                        hop(p).start()
+
+    def arrived(wanted):
+        if wanted:
+
+            @pl.when(at > copies[wanted[0]][0])
+            def _():
                 for p in wanted:
-                    hop(0, p).start()
-
-    def arrived(s, p):
-        @pl.when(at > s)
-        def _():
-            hop(s, p).wait_recv()
-
-        if s + 1 < back:
+                    hop(p).wait_recv()
+
+    def relay(count):
+        for _ in range(min(count, len(relays))):
+            s, unit = relays.pop(0)
+            arrived([p for p, c in enumerate(copies) if c[:2] == (s, unit)])
 
             @pl.when((at > s) & has_next)
             def _():
-                hop(s + 1, p).start()
-
-    relays = [(s, p) for s in range(back - 1) for p in range(len(pieces))]
-    last = [(back - 1, p) for p in range(len(pieces))] if back else []
-
-    def relay(count):
-        for _ in range(min(count, len(relays))):
-            arrived(*relays.pop(0))
+                for p, c in enumerate(copies):
+                    if c[:2] == (s + 1, unit):
+                        hop(p).start()
+
+    relays = [(s, unit) for s in range(back - 1) for unit in range(2 * (rows // block))]
 
     strip, piece = 16, 256
 
-    def norm(c):
-        @pl.loop(0, load // strip, unroll=4)
+    def norm(start, size):
+        @pl.loop(0, size // strip, unroll=4)
         def _(i):
-            here = pl.ds(pl.multiple_of(c * load + i * strip, strip), strip)
+            here = pl.ds(pl.multiple_of(start + i * strip, strip), strip)
             squares = jnp.zeros((strip, piece), F32)
             for k in range(width // piece):
                 x = xt[here, pl.ds(k * piece, piece)].astype(F32)
@@ -245,87 +272,79 @@
     def store_values(start, size, total):
         vbuf[pl.ds(mine + start, size), :] = total.astype(BF16)
 
-    high = rows - block
-    per = TQ // load
-
-    def norm_chunk(c):
-        for i in reversed(range(c * per, (c + 1) * per)):
-            norm(i)
-
-    def tok_wait(c):
-        for i in reversed(range(c * per, (c + 1) * per)):
-            tok_copy(i).wait()
-
     def weight_ready(i):
         for d in range(1, n_rows):
             weight_copy(d, i).wait_recv()
 
-    for c in reversed(range(high // TQ, tiles)):
-        tok_wait(c)
-        if c == tiles - 1:
-            small[0].wait()
-            gains[...] = jnp.broadcast_to(gain[...].astype(F32).reshape(1, -1), gains.shape)
-        norm_chunk(c)
-        if c == tiles - 1:
-            own_copy(1).start()
-            for i in reversed(range(early)):
-                tok_copy(i).start()
-            for d in range(1, n_rows):
-                weight_copy(d, 2).start()
-            small[1].start()
-            own_copy(2).start()
-    tab_copy.wait()
-    own_copy(0).wait()
+    tok_copy(0).wait()
+    small[0].wait()
+    gains[...] = jnp.broadcast_to(gain[...].astype(F32).reshape(1, -1), gains.shape)
+    norm(top + TQ // 2, TQ // 2)
+    tok_copy(1).wait()
+    norm(top, TQ // 2)
+    own_copy(1).start()
+    if high:
+        tok_copy(len(tok_parts) - 1).start()
+    for d in range(1, n_rows):
+        weight_copy(d, 2).start()
+    small[1].start()
+    own_copy(2).start()
+
     key_cols = pl.ds(0, kvw)
 
     def key_weight(d, k):
         return wkv_buf[d, pl.ds(k, half), key_cols]
 
     own = [(0, k) for k in range(0, depth, half)]
+    far = [(d, k) for d in range(1, n_rows) for k in range(0, depth, half)]
+    here = pl.ds(0, TQ)
+    own_copy(0).wait()
+    for i in near:
+        tok_copy(i).wait()
     for chain in range(2):
-        sums[chain, :, key_cols] = (
-            dots(high, block, own[chain::2], key_weight)
+        sums[chain, here, key_cols] = (
+            dots(top, TQ, own[chain::2], key_weight)
             if own[chain::2]
-            else jnp.zeros((block, kvw), F32)
+            else jnp.zeros((TQ, kvw), F32)
         )
+    for i in near:
+        norm(tok_parts[i][0], TQ)
+    tab_copy.wait()
     weight_ready(0)
-    far = [(d, k) for d in range(1, n_rows) for k in range(0, depth, half)]
-    for i in range(upper):
-        start = rows - (i + 1) * TQ
-        here = pl.ds(start - high, TQ)
-        for chain in range(2):
-            if far[chain::2]:
-                sums[chain, here, key_cols] = sums[chain, here, key_cols] + dots(
-                    start, TQ, far[chain::2], key_weight
-                )
-        store_keys(start, TQ, sums[0, here, key_cols] + sums[1, here, key_cols])
-        if i == 0 and paired:
-
-            @pl.when(has_next & jnp.logical_not(first))
-            def _():
-                pl.semaphore_wait(barrier, 2)
-                pl.semaphore_signal(ready, inc=1, device_id={"rows": 0}, device_id_type=MESH)
-
-            @pl.when(has_next & first)
-            def _():
-                pl.semaphore_wait(ready, 1)
-
-        send([i])
+    for chain in range(2):
+        if far[chain::2]:
+            sums[chain, here, key_cols] = sums[chain, here, key_cols] + dots(
+                top, TQ, far[chain::2], key_weight
+            )
+    store_keys(top, TQ, sums[0, here, key_cols] + sums[1, here, key_cols])
+    if paired:
+
+        @pl.when(has_next & jnp.logical_not(first))
+        def _():
+            pl.semaphore_wait(barrier, 2)
+            pl.semaphore_signal(ready, inc=1, device_id={"rows": 0}, device_id_type=MESH)
+
+        @pl.when(has_next & first)
+        def _():
+            pl.semaphore_wait(ready, 1)
+
+    send(0, top, TQ)
+    for i in near:
+        start = tok_parts[i][0]
+        store_keys(start, TQ, project(start, TQ, 0, kvw))
+        send(0, start, TQ)
     own_copy(1).wait()
     weight_ready(1)
     store_values(high, block, project(high, block, kvw, kvw))
-    send(range(upper, 2 * upper))
-    for c in reversed(range(high // TQ)):
-        tok_wait(c)
-    for c in reversed(range(high // TQ)):
-        norm_chunk(c)
-    sent = 2 * upper
+    send(1, high, block)
+    if high:
+        tok_copy(len(tok_parts) - 1).wait()
+        norm(0, high)
     for b in reversed(range(high // block)):
         store_keys(b * block, block, project(b * block, block, 0, kvw))
-        send(range(sent, sent + upper))
+        send(0, b * block, block)
         store_values(b * block, block, project(b * block, block, kvw, kvw))
-        send(range(sent + upper, sent + 2 * upper))
-        sent += 2 * upper
+        send(1, b * block, block)
     small[1].wait()
     for s in range(back + 1):
         owner = at - back + s
@@ -344,7 +363,7 @@
     own_copy(2).wait()
     for start in steps:
         qsum[pl.ds(start, block), :] = queries(start, 0)
-    relay(2)
+    relay(1)
     for d in range(1, n_rows):
         weight_copy(d, 2).wait_recv()
     for start in steps:
@@ -358,7 +377,7 @@
                 u = rotate(total[:, col : col + HEAD], cosine, sine)
                 for t in range(block // TQ):
                     q[start // TQ + t, h, pl.ds(g * TQ, TQ), :] = u[t * TQ : (t + 1) * TQ]
-    relay(2)
+    relay(1)
 
     factor = math.log2(math.e) / math.sqrt(HEAD)
 
@@ -427,7 +446,7 @@
         lo = reach(t, back)
         attend(t, back, lo, (t + 1) * TQ - lo, True, final(t, back, lo))
         if i % 2:
-            relay(2)
+            relay(1)
     relay(len(relays))
     for s in reversed(range(1, back)):
         for t in reversed(range(tiles)):
@@ -438,17 +457,18 @@
         for d in range(1, n_rows):
             weight_copy(d, i).wait_send()
     def come(which, start, size):
-        for s, p in last:
-            if pieces[p][0] == which and start <= pieces[p][1] < start + size:
-                arrived(s, p)
+        arrived([
+            p
+            for p, (s, _, kind, row, length) in enumerate(copies)
+            if s == back - 1 and kind == which and start < row + length <= start + size
+        ])
 
     def sent_all():
         for s in range(back):
 
             @pl.when((at >= s) & has_next)
             def _():
-                for p in range(len(pieces)):
-                    hop(s, p).wait_send()
+                all_sent(s)
 
     blocks = list(reversed(range(0, rows, block))) if back else []
     for start in blocks:
@@ -517,8 +537,8 @@
         kvw = w_key.shape[1]
         back = min(n_attn - 1, -(-(MOST - 1) // rows))
         block = 2 * TQ if rows % (2 * TQ) == 0 else rows
-        load = TQ // 2
-        pieces = 2 * (rows // TQ)
+        hops = len(hop_copies(rows, block, back))
+        near = (block - TQ) // TQ
         table = jnp.asarray(rotary_table(documents.shape[1]))
         hbm = pl.BlockSpec(memory_space=pl.ANY)
         vmem = pl.BlockSpec(memory_space=pltpu.VMEM)
@@ -526,10 +546,9 @@
         group = qw // kvw
         heads = kvw // HEAD
         tiles = rows // TQ
-        copies = 3
         args = (tokens, norm_gain, w_query, w_key, w_value, documents, table)
         return pl.pallas_call(
-            functools.partial(kernel, n_rows, n_attn, back, block, load),
+            functools.partial(kernel, n_rows, n_attn, back, block),
             out_shape=pltpu.VMEM((rows, qw), BF16),
             in_specs=[hbm] * len(args),
             out_specs=vmem,
@@ -551,12 +570,11 @@
                 pltpu.VMEM((rows, HEAD), F32),
                 pltpu.VMEM((1, keys), jnp.int32),
                 pltpu.VMEM((rows, TQ), jnp.int32),
-                pltpu.SemaphoreType.DMA((rows // load,)),
-                pltpu.SemaphoreType.DMA((copies + 3,)),
-                pltpu.SemaphoreType.DMA((n_rows, copies)),
-                pltpu.SemaphoreType.DMA((n_rows, copies)),
-                pltpu.SemaphoreType.DMA((max(back, 1), pieces)),
-                pltpu.SemaphoreType.DMA((max(back, 1), pieces)),
+                pltpu.SemaphoreType.DMA((6 + near,)),
+                pltpu.SemaphoreType.DMA((max(n_rows - 1, 1), 3)),
+                pltpu.SemaphoreType.DMA((max(n_rows - 1, 1), 3)),
+                pltpu.SemaphoreType.DMA((max(back, 1),)),
+                pltpu.SemaphoreType.DMA((max(hops, 1),)),
                 pltpu.SemaphoreType.REGULAR,
             ],
             compiler_params=pltpu.CompilerParams(

time: 17 us -> 16.7 us (0.982)
  Pallas kernels: 16.1 us -> 15.8 us
    pallas_call x1, Pallas kernels: 16.1 us -> 15.8 us  [on_device(): pl.pallas_call(functools.partial(kernel, n_rows, n_attn, back, block), ou...]
where the time goes in v5:
time: 16.7 us; the launch traced here: 16.6 us
  Pallas kernels  15.8 us (95%)
  local copies, waits for them, and re-layouts  0.8 us (5%)
    pallas_call x1, Pallas kernels, on_device(): pl.pallas_call(functools.partial(kernel, n_rows, n_attn, back, block), ou...  15.8 us
    unnamed x1, local copies, waits for them, and re-layouts  0.8 us

profile of v5, /device:TPU:18, one launch (start us, length us, event | category | flops | bytes accessed | tf_op | source)
XLA Modules:
  0.0 16.6 jit_solution(13457913630432300588)
XLA Ops:
  0.0 15.8 %layer.1 = bf16[512,512]{1,0:T(8,128)(2,1)S(1)} custom-call(bf16[512,4096]{1,0:T(8,128)(2,1)} %tok.1, bf16[4096]{0:T(1024)(128)(2,1)} %gain_in.1, bf16[2048,512]{1,0:T(8,128)(2,1)} %wq.1, bf16[2048,128]{1,0:T(8,128)(2,1)} %wk.1, bf16[2048,128]{1,0:T(8,128)(2,1)} %wv.1, s32[1,2048]{1,0:T(1,128)} %docs_in.1, f32[2048,128]{1,0:T(8,128)} %constant.2.clone.table), custom_call_target="tpu_custom_call" | custom-call | tf_op jit(solution)/shard_map/layer/pallas_call | solution.py:550
  15.8 0.8 %copy.9 = bf16[512,512]{1,0:T(8,128)(2,1)} copy(bf16[512,512]{1,0:T(8,128)(2,1)S(1)} %layer.1) | data formatting | bytes 1048576

commit v6 on v5

--- a/solution.py
+++ b/solution.py
@@ -44,7 +44,7 @@
 def kernel(
     n_rows, n_attn, back, block,
     tok, gain_in, wq, wk, wv, docs_in, table, out,
-    gain, docs, gains, xt, xn, wkv_buf, wq_buf, kbuf, vbuf, q, tops, acc, sums, qsum, tab, kdoc, qdoc,
+    gain, docs, gains, xt, xn, wkv_buf, wq_buf, kbuf, vbuf, q, tops, acc, sums, qsum, tab, kdoc, qdoc, kmask,
     own_sem, w_send, w_recv, kv_send, kv_recv, ready,
 ):
     rows, width = tok.shape
@@ -210,7 +210,11 @@
     strip, piece = 16, 256
 
     def norm(start, size):
-        @pl.loop(0, size // strip, unroll=4)
+        for first_row in reversed(range(start, start + size, 4 * strip)):
+            norm_rows(first_row)
+
+    def norm_rows(start):
+        @pl.loop(0, 4, unroll=4)
         def _(i):
             here = pl.ds(pl.multiple_of(start + i * strip, strip), strip)
             squares = jnp.zeros((strip, piece), F32)
@@ -350,9 +354,18 @@
         owner = at - back + s
         keep = pl.multiple_of(jnp.maximum(owner, 0) * rows, rows)
         kdoc[:, pl.ds(s * rows, rows)] = jnp.where(owner >= 0, docs[:, pl.ds(keep, rows)], -1)
-    for t in range(tiles):
-        row = kdoc[:, pl.ds(mine + t * TQ, TQ)]
-        qdoc[pl.ds(t * TQ, TQ), :] = jnp.broadcast_to(row, (TQ, TQ)).T
+    lanes = lax.broadcasted_iota(jnp.int32, (TQ, HEAD), 1)
+    for k in range((back + 1) * tiles):
+        here = pl.ds(k * TQ, TQ)
+        column = jnp.broadcast_to(kdoc[:, here], (HEAD, TQ)).T
+        same = column == lanes
+        kmask[here, :] = jnp.where(same, 0.0, -1e30).astype(BF16)
+        if k >= back * tiles:
+            qdoc[pl.ds((k - back * tiles) * TQ, TQ), :] = column
+            chosen = jnp.where(same, 1.0, 0.0).astype(BF16)
+            for h in range(kv_heads):
+                for g in range(group):
+                    q[k - back * tiles, h, pl.ds(g * TQ, TQ), pl.ds(HEAD, HEAD)] = chosen
 
     def queries(start, d):
         owner = lax.rem(me - d + n_rows, n_rows)
@@ -376,28 +389,38 @@
                 col = (h * group + g) * HEAD
                 u = rotate(total[:, col : col + HEAD], cosine, sine)
                 for t in range(block // TQ):
-                    q[start // TQ + t, h, pl.ds(g * TQ, TQ), :] = u[t * TQ : (t + 1) * TQ]
+                    q[start // TQ + t, h, pl.ds(g * TQ, TQ), pl.ds(0, HEAD)] = u[t * TQ : (t + 1) * TQ]
     relay(1)
 
     factor = math.log2(math.e) / math.sqrt(HEAD)
 
     def weigh(t, s, lo, size, opens):
-        seen = s * rows + lo
-        keys_at = pl.ds(seen, size)
-        visible = jnp.tile(qdoc[pl.ds(t * TQ, TQ), :], (1, size // TQ)) == kdoc[:, keys_at]
-        if s == back:
-            query_at = lax.broadcasted_iota(jnp.int32, (TQ, 1), 0) + t * TQ
-            key_at = lax.broadcasted_iota(jnp.int32, (1, size), 1) + lo
-            visible = visible & (query_at >= key_at)
+        keys_at = pl.ds(s * rows + lo, size)
         made = []
         for h in range(kv_heads):
+            keys = kbuf[keys_at, pl.ds(h * HEAD, HEAD)]
+            small = s == 0 and size == TQ
+            asked = q[t, h, :, pl.ds(0, HEAD)] if small else q[t, h]
             scores = lax.dot_general(
-                q[t, h], kbuf[keys_at, pl.ds(h * HEAD, HEAD)], (((1,), (1,)), ((), ())),
+                asked,
+                keys if small else jnp.concatenate([keys, kmask[keys_at, :]], axis=1),
+                (((1,), (1,)), ((), ())),
                 preferred_element_type=F32,
             )
-            scores = jnp.where(
-                visible[None], scores.reshape(group, TQ, size), -1e30
-            ).reshape(group * TQ, size)
+            if small:
+                seen = qdoc[pl.ds(t * TQ, TQ), :] == kdoc[:, keys_at]
+                scores = jnp.where(
+                    seen[None], scores.reshape(group, TQ, TQ), -1e30
+                ).reshape(group * TQ, TQ)
+            if s == back:
+                ahead = lanes > lax.broadcasted_iota(jnp.int32, (TQ, HEAD), 0)
+                edge = scores[:, size - TQ :].reshape(group, TQ, TQ)
+                edge = jnp.where(ahead[None], -1e30, edge).reshape(group * TQ, TQ)
+                scores = (
+                    edge
+                    if size == TQ
+                    else jnp.concatenate([scores[:, : size - TQ], edge], axis=1)
+                )
             top = jnp.broadcast_to(
                 jnp.max(scores, axis=-1, keepdims=True), (group * TQ, HEAD)
             )
@@ -562,14 +585,15 @@
                 pltpu.VMEM((n_rows, depth, qw), BF16),
                 pltpu.VMEM((keys, kvw), BF16),
                 pltpu.VMEM((keys, kvw), BF16),
-                pltpu.VMEM((tiles, heads, group * TQ, HEAD), BF16),
+                pltpu.VMEM((tiles, heads, group * TQ, 2 * HEAD), BF16),
                 pltpu.VMEM((tiles, heads, group * TQ, HEAD), F32),
                 pltpu.VMEM((tiles, heads, group * TQ, 2 * HEAD), F32),
                 pltpu.VMEM((2, block, 2 * kvw), F32),
                 pltpu.VMEM((rows, qw), F32),
                 pltpu.VMEM((rows, HEAD), F32),
                 pltpu.VMEM((1, keys), jnp.int32),
-                pltpu.VMEM((rows, TQ), jnp.int32),
+                pltpu.VMEM((rows, HEAD), jnp.int32),
+                pltpu.VMEM((keys, HEAD), BF16),
                 pltpu.SemaphoreType.DMA((6 + near,)),
                 pltpu.SemaphoreType.DMA((max(n_rows - 1, 1), 3)),
                 pltpu.SemaphoreType.DMA((max(n_rows - 1, 1), 3)),

time: 16.7 us -> 16.6 us (level)
  Pallas kernels: 15.8 us -> 15.6 us
where the time goes in v6:
time: 16.6 us; the launch traced here: 16.4 us
  Pallas kernels  15.6 us (94%)
  local copies, waits for them, and re-layouts  0.8 us (5%)
    pallas_call x1, Pallas kernels, on_device(): pl.pallas_call(functools.partial(kernel, n_rows, n_attn, back, block), ou...  15.6 us
    unnamed x1, local copies, waits for them, and re-layouts  0.8 us

profile of v6, /device:TPU:18, one launch (start us, length us, event | category | flops | bytes accessed | tf_op | source)
XLA Modules:
  0.0 16.4 jit_solution(15038203975427729898)
XLA Ops:
  0.0 15.6 %layer.1 = bf16[512,512]{1,0:T(8,128)(2,1)S(1)} custom-call(bf16[512,4096]{1,0:T(8,128)(2,1)} %tok.1, bf16[4096]{0:T(1024)(128)(2,1)} %gain_in.1, bf16[2048,512]{1,0:T(8,128)(2,1)} %wq.1, bf16[2048,128]{1,0:T(8,128)(2,1)} %wk.1, bf16[2048,128]{1,0:T(8,128)(2,1)} %wv.1, s32[1,2048]{1,0:T(1,128)} %docs_in.1, f32[2048,128]{1,0:T(8,128)} %constant.2.clone.table), custom_call_target="tpu_custom_call" | custom-call | tf_op jit(solution)/shard_map/layer/pallas_call | solution.py:573
  15.6 0.8 %copy.9 = bf16[512,512]{1,0:T(8,128)(2,1)} copy(bf16[512,512]{1,0:T(8,128)(2,1)S(1)} %layer.1) | data formatting | bytes 1048576

commit v7 on v6

--- a/solution.py
+++ b/solution.py
@@ -533,9 +533,16 @@
                 if low[t] > c:
                     continue
                 weight, carry = made[t, h, c]
-                fresh = jnp.dot(
-                    weight, vbuf[pl.ds(c, TQ), pl.ds(h * HEAD, HEAD)],
-                    preferred_element_type=F32,
+                side = group * TQ // 2
+                fresh = jnp.concatenate(
+                    [
+                        jnp.dot(
+                            weight[e : e + side], vbuf[pl.ds(c, TQ), pl.ds(h * HEAD, HEAD)],
+                            preferred_element_type=F32,
+                        )
+                        for e in (0, side)
+                    ],
+                    axis=0,
                 )
                 base[t, h] = base[t, h] + (fresh if carry is None else fresh * carry)
                 if low[t] < c:

time: 16.6 us -> 16.5 us (level)
  no operation moved by 1% of the time
where the time goes in v7:
time: 16.5 us; the launch traced here: 16.4 us
  Pallas kernels  15.6 us (95%)
  local copies, waits for them, and re-layouts  0.8 us (5%)
    pallas_call x1, Pallas kernels, on_device(): pl.pallas_call(functools.partial(kernel, n_rows, n_attn, back, block), ou...  15.6 us
    unnamed x1, local copies, waits for them, and re-layouts  0.8 us

profile of v7, /device:TPU:18, one launch (start us, length us, event | category | flops | bytes accessed | tf_op | source)
XLA Modules:
  0.0 16.4 jit_solution(5398703708775700234)
XLA Ops:
  0.0 15.6 %layer.1 = bf16[512,512]{1,0:T(8,128)(2,1)S(1)} custom-call(bf16[512,4096]{1,0:T(8,128)(2,1)} %tok.1, bf16[4096]{0:T(1024)(128)(2,1)} %gain_in.1, bf16[2048,512]{1,0:T(8,128)(2,1)} %wq.1, bf16[2048,128]{1,0:T(8,128)(2,1)} %wk.1, bf16[2048,128]{1,0:T(8,128)(2,1)} %wv.1, s32[1,2048]{1,0:T(1,128)} %docs_in.1, f32[2048,128]{1,0:T(8,128)} %constant.2.clone.table), custom_call_target="tpu_custom_call" | custom-call | tf_op jit(solution)/shard_map/layer/pallas_call | solution.py:580
  15.6 0.8 %copy.9 = bf16[512,512]{1,0:T(8,128)(2,1)} copy(bf16[512,512]{1,0:T(8,128)(2,1)S(1)} %layer.1) | data formatting | bytes 1048576

commit v8 on v7

--- a/solution.py
+++ b/solution.py
@@ -100,10 +100,10 @@
     small[0].start()
     tok_copy(0).start()
     tok_copy(1).start()
-    own_copy(0).start()
     near = range(2, 2 + (top - high) // TQ)
     for i in near:
         tok_copy(i).start()
+    own_copy(0).start()
     tab_copy.start()
 
     barrier = pltpu.get_barrier_semaphore()
@@ -302,9 +302,10 @@
     own = [(0, k) for k in range(0, depth, half)]
     far = [(d, k) for d in range(1, n_rows) for k in range(0, depth, half)]
     here = pl.ds(0, TQ)
-    own_copy(0).wait()
     for i in near:
         tok_copy(i).wait()
+        norm(tok_parts[i][0] + TQ // 2, TQ // 2)
+    own_copy(0).wait()
     for chain in range(2):
         sums[chain, here, key_cols] = (
             dots(top, TQ, own[chain::2], key_weight)
@@ -312,7 +313,7 @@
             else jnp.zeros((TQ, kvw), F32)
         )
     for i in near:
-        norm(tok_parts[i][0], TQ)
+        norm(tok_parts[i][0], TQ // 2)
     tab_copy.wait()
     weight_ready(0)
     for chain in range(2):

time: 16.5 us -> 16.5 us (level)
  no operation moved by 1% of the time
where the time goes in v8:
time: 16.5 us; the launch traced here: 16.4 us
  Pallas kernels  15.6 us (95%)
  local copies, waits for them, and re-layouts  0.8 us (5%)
    pallas_call x1, Pallas kernels, on_device(): pl.pallas_call(functools.partial(kernel, n_rows, n_attn, back, block), ou...  15.6 us
    unnamed x1, local copies, waits for them, and re-layouts  0.8 us

profile of v8, /device:TPU:18, one launch (start us, length us, event | category | flops | bytes accessed | tf_op | source)
XLA Modules:
  0.0 16.4 jit_solution(1572733009795211000)
XLA Ops:
  0.0 15.6 %layer.1 = bf16[512,512]{1,0:T(8,128)(2,1)S(1)} custom-call(bf16[512,4096]{1,0:T(8,128)(2,1)} %tok.1, bf16[4096]{0:T(1024)(128)(2,1)} %gain_in.1, bf16[2048,512]{1,0:T(8,128)(2,1)} %wq.1, bf16[2048,128]{1,0:T(8,128)(2,1)} %wk.1, bf16[2048,128]{1,0:T(8,128)(2,1)} %wv.1, s32[1,2048]{1,0:T(1,128)} %docs_in.1, f32[2048,128]{1,0:T(8,128)} %constant.2.clone.table), custom_call_target="tpu_custom_call" | custom-call | tf_op jit(solution)/shard_map/layer/pallas_call | solution.py:581
  15.6 0.8 %copy.9 = bf16[512,512]{1,0:T(8,128)(2,1)} copy(bf16[512,512]{1,0:T(8,128)(2,1)S(1)} %layer.1) | data formatting | bytes 1048576
